TPU v7x, 512 devices: a whole 4x8x8 slice. The times are simulated.
512 devices in a mesh: section: 64 (over y, x, core), dp: 8 (over z).
Axes of the slice: x: 4, y: 8, z: 8, core: 2. Of those that a mesh axis runs over, the one named last changes fastest.
Arguments:
- cotangent: bfloat16 [512, 8192], P('dp'), may hold values from -96 to 96
- lengths: int32 [16], P('dp'), may hold values from 1 to 32, as said below
- example_ids: int32 [512], P('dp'), may hold values from -1 to 15, as said below
- layer_inputs: bfloat16 [512, 32768], P('dp', 'section'), may hold values from -6 to 6
- preacts: bfloat16 [512, 32768], P('dp', 'section'), may hold values from -6 to 6
- weights: bfloat16 [32768, 8192], P('section', 'dp'), may hold values from -0.0625 to 0.0625
- query_left: bfloat16 [32768, 256], P('section'), may hold values from -0.0625 to 0.0625
- query_right: bfloat16 [32768, 256], P('section'), may hold values from -0.0625 to 0.0625
Outputs:
- input_grads: bfloat16 [512, 32768], P('dp', 'section')
- scores: float32 [16, 16], P('dp')
Inputs may be any that keep to these rules, and one draw needn't show every extreme that they name: In each aligned block of 2 sequences one length is exactly 32; the lengths of a block sum to at most 64. `example_ids`: rows n * 64 to (n + 1) * 64 - 1 hold sequences n * 2 to (n + 1) * 2 - 1 in order from the block's first row, each on as many consecutive rows as its length; the block's remaining rows hold -1.
All inputs are finite; a program needn't handle non-finite values.
Results may differ from a plain program's by a relative error of at most 0.0066.
Values may be sent and summed in bfloat16 or wider, within the bound.
A program may use at most 64 MiB of HBM per device.

v0:
```python
import jax
import jax.numpy as jnp
from jax import lax
from jax.sharding import PartitionSpec as P

LAYERS = 4
QUERIES = 16
RANK = 16
ROWS = 32


def from_partner(value, axis, distance):
    mask = 2**distance
    pairs = [(source, source ^ mask) for source in range(lax.axis_size(axis))]
    return lax.ppermute(value, axis, pairs)


def from_behind(value, axis, steps):
    count = lax.axis_size(axis)
    first, last = (max(0, -steps), min(count, count - steps))
    return lax.ppermute(value, axis, [(source, source + steps) for source in range(first, last)])


def sent_to_all(x, axis):
    copies = jnp.broadcast_to(x, (lax.axis_size(axis), *x.shape))
    return lax.all_to_all(copies, axis, split_axis=0, concat_axis=0, tiled=True)


def taken_together(x, axis):
    return sent_to_all(x, axis).sum(axis=0)


def silu_slope(preact):
    sigmoid_value = jax.nn.sigmoid(preact)
    return sigmoid_value * (1.0 + preact * (1.0 - sigmoid_value))


def per_device(
    cotangent, lengths, example_ids, layer_inputs, preacts, weights, query_left, query_right
):
    per_section = lax.axis_size("section") // LAYERS
    level_count = per_section.bit_length() - 1
    position = lax.axis_index("section")
    section_index = position // per_section
    column_block = position % per_section
    group_index = lax.axis_index("dp")
    token_count = cotangent.shape[0]
    block_cols = layer_inputs.shape[1]
    seq_count = lengths.shape[0]
    micro_count = token_count // ROWS
    step_count = LAYERS + micro_count - 1
    seq_slots = group_index * seq_count + jnp.arange(seq_count, dtype=jnp.int32)
    member = (example_ids[:, None] == seq_slots[None, :]).astype(jnp.float32)
    token_len = jnp.dot(member, lengths.astype(jnp.float32), precision=lax.Precision.HIGHEST)
    token_scale = jnp.where(example_ids >= 0, 1.0 / jnp.maximum(token_len, 1.0), 0.0)
    top_columns = lax.dynamic_slice_in_dim(cotangent, column_block * block_cols, block_cols, 1)
    top_grad = (top_columns.astype(jnp.float32) * token_scale[:, None]).astype(jnp.bfloat16)
    right_full = query_right
    for level_bit in range(level_count):
        partner = from_partner(right_full, "section", level_bit)
        upper_half = column_block >> level_bit & 1
        right_full = jnp.where(
            upper_half == 1,
            jnp.concatenate([partner, right_full], 0),
            jnp.concatenate([right_full, partner], 0),
        )
    weight_rows = lax.all_gather(weights, "dp", axis=1, tiled=True)

    def gather_gate(gate_grad):
        combined = gate_grad
        for level_bit in range(level_count):
            partner = from_partner(combined, "section", level_bit)
            upper_half = column_block >> level_bit & 1
            combined = jnp.where(
                upper_half == 1,
                jnp.concatenate([partner, combined], 1),
                jnp.concatenate([combined, partner], 1),
            )
        return combined

    def score_terms(gate_full, input_rows, id_rows):
        left_part = jnp.dot(input_rows, query_left, preferred_element_type=jnp.float32)
        right_part = jnp.dot(gate_full, right_full, preferred_element_type=jnp.float32)
        per_token = jnp.sum((left_part * right_part).reshape(ROWS, QUERIES, RANK), axis=2)
        block_member = (id_rows[:, None] == seq_slots[None, :]).astype(jnp.float32)
        return jnp.dot(block_member.T, per_token, precision=lax.Precision.HIGHEST)

    def advance(clock_tick, loop_state):
        outgoing, grad_store, totals = loop_state
        arrived = from_behind(outgoing, "section", -per_section)
        micro_index = clock_tick - (LAYERS - 1 - section_index)
        in_range = (micro_index >= 0) & (micro_index < micro_count)
        row_start = jnp.clip(micro_index, 0, micro_count - 1) * ROWS
        top_rows = lax.dynamic_slice_in_dim(top_grad, row_start, ROWS, 0)
        grad_out = jnp.where(section_index == LAYERS - 1, top_rows, arrived)
        preact = lax.dynamic_slice_in_dim(preacts, row_start, ROWS, 0).astype(jnp.float32)
        gate_grad = (silu_slope(preact) * grad_out.astype(jnp.float32)).astype(jnp.bfloat16)
        gate_full = gather_gate(gate_grad)
        input_rows = lax.dynamic_slice_in_dim(layer_inputs, row_start, ROWS, 0)
        id_rows = lax.dynamic_slice_in_dim(example_ids, row_start, ROWS, 0)
        has_live = in_range & jnp.any(id_rows >= 0)

        def project():
            return lax.dot_general(
                gate_full, weight_rows, (((1,), (1,)), ((), ())), preferred_element_type=jnp.float32
            )

        def scoring():
            return score_terms(gate_full, input_rows, id_rows)

        backward = lax.cond(has_live, project, lambda: jnp.zeros((ROWS, block_cols), jnp.float32))
        increment = lax.cond(
            has_live, scoring, lambda: jnp.zeros((seq_count, QUERIES), jnp.float32)
        )
        in_grad = (grad_out.astype(jnp.float32) + backward).astype(jnp.bfloat16)
        updated = lax.dynamic_update_slice_in_dim(grad_store, in_grad, row_start, 0)
        grad_store = jnp.where(in_range, updated, grad_store)
        increment = jnp.where(in_range, increment, 0.0)
        totals = totals + increment
        return (in_grad, grad_store, totals)

    initial = (
        jnp.zeros((ROWS, block_cols), jnp.bfloat16),
        jnp.zeros((token_count, block_cols), jnp.bfloat16),
        jnp.zeros((seq_count, QUERIES), jnp.float32),
    )
    outgoing, grad_store, totals = lax.fori_loop(0, step_count, advance, initial)
    totals = taken_together(totals, "section")
    return (grad_store, totals)


def solution(mesh):
    placed = (
        P("dp", None),
        P("dp"),
        P("dp"),
        P("dp", "section"),
        P("dp", "section"),
        P("section", "dp"),
        P("section", None),
        P("section", None),
    )
    return jax.shard_map(
        per_device,
        mesh=mesh,
        in_specs=placed,
        out_specs=(P("dp", "section"), P("dp", None)),
        check_vma=False,
    )
```

profile of v0, /device:TPU:1, one launch (start us, length us, event | category | flops | bytes accessed | tf_op | source)
XLA Modules:
  0.0 347.1 jit_solution(5726341101719994201)
XLA Ops:
  7.9 8.7 %collective-permute-start.5 = (bf16[512,256]{1,0:T(8,128)(2,1)}, bf16[512,256]{1,0:T(8,128)(2,1)S(1)}, u32[]{:S(2)}, u32[]{:S(2)}) collective-permute-start(bf16[512,256]{1,0:T(8,128)(2,1)} %param.21), channel_id=1, source_target_pairs={{0,8},{8,0},{16,24},{24,16},{32,40},{40,32},{48,56},{56,48},{64,72... | collective-permute-start | bytes 786440 | tf_op jit(solution)/shard_map/ppermute | solution.py:15
  21.2 13.2 %collective-permute-done.6 = bf16[1024,256]{1,0:T(8,128)(2,1)S(1)} collective-permute-done((bf16[1024,256]{1,0:T(8,128)(2,1)S(1)}, bf16[1024,256]{1,0:T(8,128)(2,1)S(1)}, u32[]{:S(2)}, u32[]{:S(2)}) %collective-permute-start.6) | collective-permute-done | bytes 524320 | tf_op jit(solution)/shard_map/ppermute | solution.py:15
  36.6 25.2 %collective-permute-done.7 = bf16[2048,256]{1,0:T(8,128)(2,1)} collective-permute-done((bf16[2048,256]{1,0:T(8,128)(2,1)S(1)}, bf16[2048,256]{1,0:T(8,128)(2,1)}, u32[]{:S(2)}, u32[]{:S(2)}) %collective-permute-start.7) | collective-permute-done | bytes 1048608 | tf_op jit(solution)/shard_map/ppermute | solution.py:15
  67.1 44.0 %collective-permute-done.8 = bf16[4096,256]{1,0:T(8,128)(2,1)} collective-permute-done((bf16[4096,256]{1,0:T(8,128)(2,1)S(1)}, bf16[4096,256]{1,0:T(8,128)(2,1)}, u32[]{:S(2)}, u32[]{:S(2)}) %collective-permute-start.8) | collective-permute-done | bytes 2097184 | tf_op jit(solution)/shard_map/ppermute | solution.py:15
  111.1 4.2 %maximum_select_fusion.4 = bf16[8192,256]{1,0:T(8,128)(2,1)} fusion(bf16[4096,256]{1,0:T(8,128)(2,1)S(1)} %maximum_select_fusion.5, bf16[4096,256]{1,0:T(8,128)(2,1)} %collective-permute-done.8, pred[]{:T(512)} %eq.84), kind=kLoop, calls=%fused_computation.31 | loop fusion | flops 18874368 | bytes 8388609 | tf_op jit(solution)/shard_map/jit(_where)/select_n | solution.py:62
  115.4 205.7 %while.20 = (s32[]{:T(128)}, bf16[32,512]{1,0:T(8,128)(2,1)S(1)}, bf16[64,512]{1,0:T(8,128)(2,1)S(1)}, f32[2,16]{1,0:T(2,128)S(1)}, pred[]{:T(512)}, /*index=5*/...) while((s32[]{:T(128)}, bf16[32,512]{1,0:T(8,128)(2,1)S(1)}, ...), condition=%wide.region_7.8_spmd.clone, body=%wide.region_0.7_spmd.clone.sunk | while | flops 415788832 | bytes 18683436 | solution.py:127
  116.7 4.6 %collective-permute-done = bf16[32,512]{1,0:T(8,128)(2,1)S(1)} collective-permute-done((bf16[32,512]{1,0:T(8,128)(2,1)S(1)}, bf16[32,512]{1,0:T(8,128)(2,1)S(1)}, u32[]{:S(2)}, u32[]{:S(2)}) %collective-permute-start) | collective-permute-done | bytes 32800 | tf_op jit(solution)/shard_map/while/body/eval_jaxpr/ppermute | solution.py:21
  121.3 5.6 %collective-permute-start.1 = (bf16[32,512]{1,0:T(8,128)(2,1)S(1)}, bf16[32,512]{1,0:T(8,128)(2,1)S(1)}, u32[]{:S(2)}, u32[]{:S(2)}) collective-permute-start(bf16[32,512]{1,0:T(8,128)(2,1)S(1)} %fusion.30), channel_id=1, source_target_pairs={{0,8},{8,0},{16,24},{24,16},{32,40},{40,32},{48,56},{56,48},{64,72... | collective-permute-start | bytes 98312 | tf_op jit(solution)/shard_map/while/body/eval_jaxpr/ppermute | solution.py:15
  135.2 4.9 %collective-permute-done.3 = bf16[32,2048]{1,0:T(8,128)(2,1)S(1)} collective-permute-done((bf16[32,2048]{1,0:T(8,128)(2,1)S(1)}, bf16[32,2048]{1,0:T(8,128)(2,1)S(1)}, u32[]{:S(2)}, u32[]{:S(2)}) %collective-permute-start.3) | collective-permute-done | bytes 131104 | tf_op jit(solution)/shard_map/while/body/eval_jaxpr/ppermute | solution.py:15
  143.6 3.7 %collective-permute-done.4 = bf16[32,4096]{1,0:T(8,128)(2,1)S(1)} collective-permute-done((bf16[32,4096]{1,0:T(8,128)(2,1)S(1)}, bf16[32,4096]{1,0:T(8,128)(2,1)S(1)}, u32[]{:S(2)}, u32[]{:S(2)}) %collective-permute-start.4) | collective-permute-done | bytes 262176 | tf_op jit(solution)/shard_map/while/body/eval_jaxpr/ppermute | solution.py:15
  148.9 4.3 %collective-permute-done = bf16[32,512]{1,0:T(8,128)(2,1)S(1)} collective-permute-done((bf16[32,512]{1,0:T(8,128)(2,1)S(1)}, bf16[32,512]{1,0:T(8,128)(2,1)S(1)}, u32[]{:S(2)}, u32[]{:S(2)}) %collective-permute-start) | collective-permute-done | bytes 32800 | tf_op jit(solution)/shard_map/while/body/eval_jaxpr/ppermute | solution.py:21
  153.3 6.8 %collective-permute-start.1 = (bf16[32,512]{1,0:T(8,128)(2,1)S(1)}, bf16[32,512]{1,0:T(8,128)(2,1)S(1)}, u32[]{:S(2)}, u32[]{:S(2)}) collective-permute-start(bf16[32,512]{1,0:T(8,128)(2,1)S(1)} %fusion.30), channel_id=1, source_target_pairs={{0,8},{8,0},{16,24},{24,16},{32,40},{40,32},{48,56},{56,48},{64,72... | collective-permute-start | bytes 98312 | tf_op jit(solution)/shard_map/while/body/eval_jaxpr/ppermute | solution.py:15
  168.6 4.6 %collective-permute-done.3 = bf16[32,2048]{1,0:T(8,128)(2,1)S(1)} collective-permute-done((bf16[32,2048]{1,0:T(8,128)(2,1)S(1)}, bf16[32,2048]{1,0:T(8,128)(2,1)S(1)}, u32[]{:S(2)}, u32[]{:S(2)}) %collective-permute-start.3) | collective-permute-done | bytes 131104 | tf_op jit(solution)/shard_map/while/body/eval_jaxpr/ppermute | solution.py:15
  176.7 3.7 %collective-permute-done.4 = bf16[32,4096]{1,0:T(8,128)(2,1)S(1)} collective-permute-done((bf16[32,4096]{1,0:T(8,128)(2,1)S(1)}, bf16[32,4096]{1,0:T(8,128)(2,1)S(1)}, u32[]{:S(2)}, u32[]{:S(2)}) %collective-permute-start.4) | collective-permute-done | bytes 262176 | tf_op jit(solution)/shard_map/while/body/eval_jaxpr/ppermute | solution.py:15
  182.0 4.3 %collective-permute-done = bf16[32,512]{1,0:T(8,128)(2,1)S(1)} collective-permute-done((bf16[32,512]{1,0:T(8,128)(2,1)S(1)}, bf16[32,512]{1,0:T(8,128)(2,1)S(1)}, u32[]{:S(2)}, u32[]{:S(2)}) %collective-permute-start) | collective-permute-done | bytes 32800 | tf_op jit(solution)/shard_map/while/body/eval_jaxpr/ppermute | solution.py:21
  186.3 6.8 %collective-permute-start.1 = (bf16[32,512]{1,0:T(8,128)(2,1)S(1)}, bf16[32,512]{1,0:T(8,128)(2,1)S(1)}, u32[]{:S(2)}, u32[]{:S(2)}) collective-permute-start(bf16[32,512]{1,0:T(8,128)(2,1)S(1)} %fusion.30), channel_id=1, source_target_pairs={{0,8},{8,0},{16,24},{24,16},{32,40},{40,32},{48,56},{56,48},{64,72... | collective-permute-start | bytes 98312 | tf_op jit(solution)/shard_map/while/body/eval_jaxpr/ppermute | solution.py:15
  201.7 4.6 %collective-permute-done.3 = bf16[32,2048]{1,0:T(8,128)(2,1)S(1)} collective-permute-done((bf16[32,2048]{1,0:T(8,128)(2,1)S(1)}, bf16[32,2048]{1,0:T(8,128)(2,1)S(1)}, u32[]{:S(2)}, u32[]{:S(2)}) %collective-permute-start.3) | collective-permute-done | bytes 131104 | tf_op jit(solution)/shard_map/while/body/eval_jaxpr/ppermute | solution.py:15
  209.7 3.7 %collective-permute-done.4 = bf16[32,4096]{1,0:T(8,128)(2,1)S(1)} collective-permute-done((bf16[32,4096]{1,0:T(8,128)(2,1)S(1)}, bf16[32,4096]{1,0:T(8,128)(2,1)S(1)}, u32[]{:S(2)}, u32[]{:S(2)}) %collective-permute-start.4) | collective-permute-done | bytes 262176 | tf_op jit(solution)/shard_map/while/body/eval_jaxpr/ppermute | solution.py:15
  215.0 25.5 %collective-permute-done = bf16[32,512]{1,0:T(8,128)(2,1)S(1)} collective-permute-done((bf16[32,512]{1,0:T(8,128)(2,1)S(1)}, bf16[32,512]{1,0:T(8,128)(2,1)S(1)}, u32[]{:S(2)}, u32[]{:S(2)}) %collective-permute-start) | collective-permute-done | bytes 32800 | tf_op jit(solution)/shard_map/while/body/eval_jaxpr/ppermute | solution.py:21
  240.5 6.6 %collective-permute-start.1 = (bf16[32,512]{1,0:T(8,128)(2,1)S(1)}, bf16[32,512]{1,0:T(8,128)(2,1)S(1)}, u32[]{:S(2)}, u32[]{:S(2)}) collective-permute-start(bf16[32,512]{1,0:T(8,128)(2,1)S(1)} %fusion.30), channel_id=1, source_target_pairs={{0,8},{8,0},{16,24},{24,16},{32,40},{40,32},{48,56},{56,48},{64,72... | collective-permute-start | bytes 98312 | tf_op jit(solution)/shard_map/while/body/eval_jaxpr/ppermute | solution.py:15
  253.0 4.6 %collective-permute-start.3 = (bf16[32,2048]{1,0:T(8,128)(2,1)S(1)}, bf16[32,2048]{1,0:T(8,128)(2,1)S(1)}, u32[]{:S(2)}, u32[]{:S(2)}) collective-permute-start(bf16[32,2048]{1,0:T(8,128)(2,1)S(1)} %maximum_select_fusion.13), channel_id=1, source_target_pairs={{0,32},{8,40},{16,48},{24,56},{32,0},{40,8},{48,16},{56,24},{64,96... | collective-permute-start | bytes 393224 | tf_op jit(solution)/shard_map/while/body/eval_jaxpr/ppermute | solution.py:15
  263.7 3.7 %collective-permute-done.4 = bf16[32,4096]{1,0:T(8,128)(2,1)S(1)} collective-permute-done((bf16[32,4096]{1,0:T(8,128)(2,1)S(1)}, bf16[32,4096]{1,0:T(8,128)(2,1)S(1)}, u32[]{:S(2)}, u32[]{:S(2)}) %collective-permute-start.4) | collective-permute-done | bytes 262176 | tf_op jit(solution)/shard_map/while/body/eval_jaxpr/ppermute | solution.py:15
  267.6 6.0 %conditional.6 = (f32[32,512]{1,0:T(8,128)S(1)}) conditional(s32[]{:T(128)} %convert_element_type.103, () %tuple.71, (bf16[32,8192]{1,0:T(8,128)(2,1)S(1)}, bf16[512,8192]{1,0:T(8,128)(2,1)}) %tuple.72), branch_computations={%region_2.2_spmd, %region_3.3_spmd} | conditional | flops 268435456 | bytes 8978440 | solution.py:111
  267.6 6.0 %fusion.22 = f32[32,512]{1,0:T(8,128)S(1)} fusion(bf16[32,8192]{1,0:T(8,128)(2,1)S(1)} %get-tuple-element.379, bf16[512,8192]{1,0:T(8,128)(2,1)} %get-tuple-element.380), kind=kOutput, calls=%fused_computation.45 | convolution fusion | flops 268435456 | bytes 8978432 | tf_op jit(solution)/shard_map/while/body/eval_jaxpr/cond/branch_1_fun/dot_general | solution.py:104
  278.6 5.7 %collective-permute-done = bf16[32,512]{1,0:T(8,128)(2,1)S(1)} collective-permute-done((bf16[32,512]{1,0:T(8,128)(2,1)S(1)}, bf16[32,512]{1,0:T(8,128)(2,1)S(1)}, u32[]{:S(2)}, u32[]{:S(2)}) %collective-permute-start) | collective-permute-done | bytes 32800 | tf_op jit(solution)/shard_map/while/body/eval_jaxpr/ppermute | solution.py:21
  284.3 6.6 %collective-permute-start.1 = (bf16[32,512]{1,0:T(8,128)(2,1)S(1)}, bf16[32,512]{1,0:T(8,128)(2,1)S(1)}, u32[]{:S(2)}, u32[]{:S(2)}) collective-permute-start(bf16[32,512]{1,0:T(8,128)(2,1)S(1)} %fusion.30), channel_id=1, source_target_pairs={{0,8},{8,0},{16,24},{24,16},{32,40},{40,32},{48,56},{56,48},{64,72... | collective-permute-start | bytes 98312 | tf_op jit(solution)/shard_map/while/body/eval_jaxpr/ppermute | solution.py:15
  296.8 4.6 %collective-permute-start.3 = (bf16[32,2048]{1,0:T(8,128)(2,1)S(1)}, bf16[32,2048]{1,0:T(8,128)(2,1)S(1)}, u32[]{:S(2)}, u32[]{:S(2)}) collective-permute-start(bf16[32,2048]{1,0:T(8,128)(2,1)S(1)} %maximum_select_fusion.13), channel_id=1, source_target_pairs={{0,32},{8,40},{16,48},{24,56},{32,0},{40,8},{48,16},{56,24},{64,96... | collective-permute-start | bytes 393224 | tf_op jit(solution)/shard_map/while/body/eval_jaxpr/ppermute | solution.py:15
  307.5 3.7 %collective-permute-done.4 = bf16[32,4096]{1,0:T(8,128)(2,1)S(1)} collective-permute-done((bf16[32,4096]{1,0:T(8,128)(2,1)S(1)}, bf16[32,4096]{1,0:T(8,128)(2,1)S(1)}, u32[]{:S(2)}, u32[]{:S(2)}) %collective-permute-start.4) | collective-permute-done | bytes 262176 | tf_op jit(solution)/shard_map/while/body/eval_jaxpr/ppermute | solution.py:15
  311.4 6.0 %conditional.6 = (f32[32,512]{1,0:T(8,128)S(1)}) conditional(s32[]{:T(128)} %convert_element_type.103, () %tuple.71, (bf16[32,8192]{1,0:T(8,128)(2,1)S(1)}, bf16[512,8192]{1,0:T(8,128)(2,1)}) %tuple.72), branch_computations={%region_2.2_spmd, %region_3.3_spmd} | conditional | flops 268435456 | bytes 8978440 | solution.py:111
  311.4 6.0 %fusion.22 = f32[32,512]{1,0:T(8,128)S(1)} fusion(bf16[32,8192]{1,0:T(8,128)(2,1)S(1)} %get-tuple-element.379, bf16[512,8192]{1,0:T(8,128)(2,1)} %get-tuple-element.380), kind=kOutput, calls=%fused_computation.45 | convolution fusion | flops 268435456 | bytes 8978432 | tf_op jit(solution)/shard_map/while/body/eval_jaxpr/cond/branch_1_fun/dot_general | solution.py:104
  317.4 3.6 %conditional.7 = (f32[2,16]{1,0:T(2,128)S(1)}) conditional(s32[]{:T(128)} %convert_element_type.103, () %tuple.73, (s32[32]{0:T(128)S(1)}, s32[]{:T(128)}, bf16[64,512]{1,0:T(8,128)(2,1)S(1)}, s32[]{:T(128)}, bf16[512,256]{1,0:T(8,128)(2,1)S(1)}, /*index=5*/bf16[32,8192]{1,0:T(8,128)(2,1)S(1)}, bf16[8192,256]{1,0:T(8,128)(2,1)}, s32[2]{0:T(128)S(1)}) %tuple.74), branch_computations={%region_4.4_spmd, %region_5.6_spmd} | conditional | flops 142634624 | bytes 5214504 | solution.py:112
  321.1 18.5 %all_to_all.5 = f32[64,2,16]{2,1,0:T(2,128)S(1)} all-to-all(f32[64,2,16]{2,1,0:T(2,128)S(1)} %broadcast_in_dim.31), channel_id=1, replica_groups=mesh['section'=64,'dp'=8] {'section'}, dimensions={0} | all-to-all | bytes 16384 | tf_op jit(solution)/shard_map/all_to_all | solution.py:26
  (135 shorter events, 87.9 us)
Async XLA Ops:
  7.2 58.7 %copy-start.5 = (s32[2]{0:T(128)S(1)}, s32[2]{0:T(128)}, u32[]{:S(2)}) copy-start(s32[2]{0:T(128)} %param.15) | copy-start | bytes 28
  7.2 58.7 %copy-start.4 = (s32[64]{0:T(128)S(1)}, s32[64]{0:T(128)}, u32[]{:S(2)}) copy-start(s32[64]{0:T(128)} %param.16) | copy-start | bytes 772
  7.2 108.1 %all-gather.2.cloned.1.call-start = ((), (), s32[]{:S(2)}) async-start(), calls=%async_computation.1 | async-start | bytes 9437184 | tf_op jit(solution)/shard_map/all_gather | solution.py:67
  7.9 10.1 %collective-permute-start.5 = (bf16[512,256]{1,0:T(8,128)(2,1)}, bf16[512,256]{1,0:T(8,128)(2,1)S(1)}, u32[]{:S(2)}, u32[]{:S(2)}) collective-permute-start(bf16[512,256]{1,0:T(8,128)(2,1)} %param.21), channel_id=1, source_target_pairs={{0,8},{8,0},{16,24},{24,16},{32,40},{40,32},{48,56},{56,48},{64,72... | collective-permute-start | bytes 786440 | tf_op jit(solution)/shard_map/ppermute | solution.py:15
  19.3 15.1 %collective-permute-start.6 = (bf16[1024,256]{1,0:T(8,128)(2,1)S(1)}, bf16[1024,256]{1,0:T(8,128)(2,1)S(1)}, u32[]{:S(2)}, u32[]{:S(2)}) collective-permute-start(bf16[1024,256]{1,0:T(8,128)(2,1)S(1)} %maximum_select_fusion.7), channel_id=1, source_target_pairs={{0,16},{8,24},{16,0},{24,8},{32,48},{40,56},{48,32},{56,40},{64,80... | collective-permute-start | bytes 1572872 | tf_op jit(solution)/shard_map/ppermute | solution.py:15
  34.6 27.1 %collective-permute-start.7 = (bf16[2048,256]{1,0:T(8,128)(2,1)S(1)}, bf16[2048,256]{1,0:T(8,128)(2,1)}, u32[]{:S(2)}, u32[]{:S(2)}) collective-permute-start(bf16[2048,256]{1,0:T(8,128)(2,1)S(1)} %maximum_select_fusion.6), channel_id=1, source_target_pairs={{0,32},{8,40},{16,48},{24,56},{32,0},{40,8},{48,16},{56,24},{64,96... | collective-permute-start | bytes 3145736 | tf_op jit(solution)/shard_map/ppermute | solution.py:15
  63.9 47.2 %collective-permute-start.8 = (bf16[4096,256]{1,0:T(8,128)(2,1)S(1)}, bf16[4096,256]{1,0:T(8,128)(2,1)}, u32[]{:S(2)}, u32[]{:S(2)}) collective-permute-start(bf16[4096,256]{1,0:T(8,128)(2,1)S(1)} %maximum_select_fusion.5), channel_id=1, source_target_pairs={{0,64},{8,72},{16,80},{24,88},{32,96},{40,104},{48,112},{56,120},{... | collective-permute-start | bytes 6291464 | tf_op jit(solution)/shard_map/ppermute | solution.py:15
  115.4 5.9 %collective-permute-start = (bf16[32,512]{1,0:T(8,128)(2,1)S(1)}, bf16[32,512]{1,0:T(8,128)(2,1)S(1)}, u32[]{:S(2)}, u32[]{:S(2)}) collective-permute-start(bf16[32,512]{1,0:T(8,128)(2,1)S(1)} %broadcast_select_fusion.2), channel_id=1, source_target_pairs={{128,0},{136,8},{144,16},{152,24},{160,32},{168,40},{176,48},{184,... | collective-permute-start | bytes 98312 | tf_op jit(solution)/shard_map/while/body/eval_jaxpr/ppermute | solution.py:21
  121.3 6.5 %collective-permute-start.1 = (bf16[32,512]{1,0:T(8,128)(2,1)S(1)}, bf16[32,512]{1,0:T(8,128)(2,1)S(1)}, u32[]{:S(2)}, u32[]{:S(2)}) collective-permute-start(bf16[32,512]{1,0:T(8,128)(2,1)S(1)} %fusion.30), channel_id=1, source_target_pairs={{0,8},{8,0},{16,24},{24,16},{32,40},{40,32},{48,56},{56,48},{64,72... | collective-permute-start | bytes 98312 | tf_op jit(solution)/shard_map/while/body/eval_jaxpr/ppermute | solution.py:15
  127.8 5.0 %collective-permute-start.2 = (bf16[32,1024]{1,0:T(8,128)(2,1)S(1)}, bf16[32,1024]{1,0:T(8,128)(2,1)S(1)}, u32[]{:S(2)}, u32[]{:S(2)}) collective-permute-start(bf16[32,1024]{1,0:T(8,128)(2,1)S(1)} %maximum_select_fusion.12), channel_id=1, source_target_pairs={{0,16},{8,24},{16,0},{24,8},{32,48},{40,56},{48,32},{56,40},{64,80... | collective-permute-start | bytes 196616 | tf_op jit(solution)/shard_map/while/body/eval_jaxpr/ppermute | solution.py:15
  132.9 7.2 %collective-permute-start.3 = (bf16[32,2048]{1,0:T(8,128)(2,1)S(1)}, bf16[32,2048]{1,0:T(8,128)(2,1)S(1)}, u32[]{:S(2)}, u32[]{:S(2)}) collective-permute-start(bf16[32,2048]{1,0:T(8,128)(2,1)S(1)} %maximum_select_fusion.13), channel_id=1, source_target_pairs={{0,32},{8,40},{16,48},{24,56},{32,0},{40,8},{48,16},{56,24},{64,96... | collective-permute-start | bytes 393224 | tf_op jit(solution)/shard_map/while/body/eval_jaxpr/ppermute | solution.py:15
  140.2 7.1 %collective-permute-start.4 = (bf16[32,4096]{1,0:T(8,128)(2,1)S(1)}, bf16[32,4096]{1,0:T(8,128)(2,1)S(1)}, u32[]{:S(2)}, u32[]{:S(2)}) collective-permute-start(bf16[32,4096]{1,0:T(8,128)(2,1)S(1)} %maximum_select_fusion.14), channel_id=1, source_target_pairs={{0,64},{8,72},{16,80},{24,88},{32,96},{40,104},{48,112},{56,120},{... | collective-permute-start | bytes 786440 | tf_op jit(solution)/shard_map/while/body/eval_jaxpr/ppermute | solution.py:15
  147.6 5.6 %collective-permute-start = (bf16[32,512]{1,0:T(8,128)(2,1)S(1)}, bf16[32,512]{1,0:T(8,128)(2,1)S(1)}, u32[]{:S(2)}, u32[]{:S(2)}) collective-permute-start(bf16[32,512]{1,0:T(8,128)(2,1)S(1)} %broadcast_select_fusion.2), channel_id=1, source_target_pairs={{128,0},{136,8},{144,16},{152,24},{160,32},{168,40},{176,48},{184,... | collective-permute-start | bytes 98312 | tf_op jit(solution)/shard_map/while/body/eval_jaxpr/ppermute | solution.py:21
  153.3 7.6 %collective-permute-start.1 = (bf16[32,512]{1,0:T(8,128)(2,1)S(1)}, bf16[32,512]{1,0:T(8,128)(2,1)S(1)}, u32[]{:S(2)}, u32[]{:S(2)}) collective-permute-start(bf16[32,512]{1,0:T(8,128)(2,1)S(1)} %fusion.30), channel_id=1, source_target_pairs={{0,8},{8,0},{16,24},{24,16},{32,40},{40,32},{48,56},{56,48},{64,72... | collective-permute-start | bytes 98312 | tf_op jit(solution)/shard_map/while/body/eval_jaxpr/ppermute | solution.py:15
  160.9 5.0 %collective-permute-start.2 = (bf16[32,1024]{1,0:T(8,128)(2,1)S(1)}, bf16[32,1024]{1,0:T(8,128)(2,1)S(1)}, u32[]{:S(2)}, u32[]{:S(2)}) collective-permute-start(bf16[32,1024]{1,0:T(8,128)(2,1)S(1)} %maximum_select_fusion.12), channel_id=1, source_target_pairs={{0,16},{8,24},{16,0},{24,8},{32,48},{40,56},{48,32},{56,40},{64,80... | collective-permute-start | bytes 196616 | tf_op jit(solution)/shard_map/while/body/eval_jaxpr/ppermute | solution.py:15
  165.9 7.2 %collective-permute-start.3 = (bf16[32,2048]{1,0:T(8,128)(2,1)S(1)}, bf16[32,2048]{1,0:T(8,128)(2,1)S(1)}, u32[]{:S(2)}, u32[]{:S(2)}) collective-permute-start(bf16[32,2048]{1,0:T(8,128)(2,1)S(1)} %maximum_select_fusion.13), channel_id=1, source_target_pairs={{0,32},{8,40},{16,48},{24,56},{32,0},{40,8},{48,16},{56,24},{64,96... | collective-permute-start | bytes 393224 | tf_op jit(solution)/shard_map/while/body/eval_jaxpr/ppermute | solution.py:15
  173.2 7.1 %collective-permute-start.4 = (bf16[32,4096]{1,0:T(8,128)(2,1)S(1)}, bf16[32,4096]{1,0:T(8,128)(2,1)S(1)}, u32[]{:S(2)}, u32[]{:S(2)}) collective-permute-start(bf16[32,4096]{1,0:T(8,128)(2,1)S(1)} %maximum_select_fusion.14), channel_id=1, source_target_pairs={{0,64},{8,72},{16,80},{24,88},{32,96},{40,104},{48,112},{56,120},{... | collective-permute-start | bytes 786440 | tf_op jit(solution)/shard_map/while/body/eval_jaxpr/ppermute | solution.py:15
  180.6 5.6 %collective-permute-start = (bf16[32,512]{1,0:T(8,128)(2,1)S(1)}, bf16[32,512]{1,0:T(8,128)(2,1)S(1)}, u32[]{:S(2)}, u32[]{:S(2)}) collective-permute-start(bf16[32,512]{1,0:T(8,128)(2,1)S(1)} %broadcast_select_fusion.2), channel_id=1, source_target_pairs={{128,0},{136,8},{144,16},{152,24},{160,32},{168,40},{176,48},{184,... | collective-permute-start | bytes 98312 | tf_op jit(solution)/shard_map/while/body/eval_jaxpr/ppermute | solution.py:21
  186.3 7.6 %collective-permute-start.1 = (bf16[32,512]{1,0:T(8,128)(2,1)S(1)}, bf16[32,512]{1,0:T(8,128)(2,1)S(1)}, u32[]{:S(2)}, u32[]{:S(2)}) collective-permute-start(bf16[32,512]{1,0:T(8,128)(2,1)S(1)} %fusion.30), channel_id=1, source_target_pairs={{0,8},{8,0},{16,24},{24,16},{32,40},{40,32},{48,56},{56,48},{64,72... | collective-permute-start | bytes 98312 | tf_op jit(solution)/shard_map/while/body/eval_jaxpr/ppermute | solution.py:15
  194.0 5.0 %collective-permute-start.2 = (bf16[32,1024]{1,0:T(8,128)(2,1)S(1)}, bf16[32,1024]{1,0:T(8,128)(2,1)S(1)}, u32[]{:S(2)}, u32[]{:S(2)}) collective-permute-start(bf16[32,1024]{1,0:T(8,128)(2,1)S(1)} %maximum_select_fusion.12), channel_id=1, source_target_pairs={{0,16},{8,24},{16,0},{24,8},{32,48},{40,56},{48,32},{56,40},{64,80... | collective-permute-start | bytes 196616 | tf_op jit(solution)/shard_map/while/body/eval_jaxpr/ppermute | solution.py:15
  199.0 7.2 %collective-permute-start.3 = (bf16[32,2048]{1,0:T(8,128)(2,1)S(1)}, bf16[32,2048]{1,0:T(8,128)(2,1)S(1)}, u32[]{:S(2)}, u32[]{:S(2)}) collective-permute-start(bf16[32,2048]{1,0:T(8,128)(2,1)S(1)} %maximum_select_fusion.13), channel_id=1, source_target_pairs={{0,32},{8,40},{16,48},{24,56},{32,0},{40,8},{48,16},{56,24},{64,96... | collective-permute-start | bytes 393224 | tf_op jit(solution)/shard_map/while/body/eval_jaxpr/ppermute | solution.py:15
  206.3 7.1 %collective-permute-start.4 = (bf16[32,4096]{1,0:T(8,128)(2,1)S(1)}, bf16[32,4096]{1,0:T(8,128)(2,1)S(1)}, u32[]{:S(2)}, u32[]{:S(2)}) collective-permute-start(bf16[32,4096]{1,0:T(8,128)(2,1)S(1)} %maximum_select_fusion.14), channel_id=1, source_target_pairs={{0,64},{8,72},{16,80},{24,88},{32,96},{40,104},{48,112},{56,120},{... | collective-permute-start | bytes 786440 | tf_op jit(solution)/shard_map/while/body/eval_jaxpr/ppermute | solution.py:15
  213.7 26.8 %collective-permute-start = (bf16[32,512]{1,0:T(8,128)(2,1)S(1)}, bf16[32,512]{1,0:T(8,128)(2,1)S(1)}, u32[]{:S(2)}, u32[]{:S(2)}) collective-permute-start(bf16[32,512]{1,0:T(8,128)(2,1)S(1)} %broadcast_select_fusion.2), channel_id=1, source_target_pairs={{128,0},{136,8},{144,16},{152,24},{160,32},{168,40},{176,48},{184,... | collective-permute-start | bytes 98312 | tf_op jit(solution)/shard_map/while/body/eval_jaxpr/ppermute | solution.py:21
  240.5 7.4 %collective-permute-start.1 = (bf16[32,512]{1,0:T(8,128)(2,1)S(1)}, bf16[32,512]{1,0:T(8,128)(2,1)S(1)}, u32[]{:S(2)}, u32[]{:S(2)}) collective-permute-start(bf16[32,512]{1,0:T(8,128)(2,1)S(1)} %fusion.30), channel_id=1, source_target_pairs={{0,8},{8,0},{16,24},{24,16},{32,40},{40,32},{48,56},{56,48},{64,72... | collective-permute-start | bytes 98312 | tf_op jit(solution)/shard_map/while/body/eval_jaxpr/ppermute | solution.py:15
  248.0 5.0 %collective-permute-start.2 = (bf16[32,1024]{1,0:T(8,128)(2,1)S(1)}, bf16[32,1024]{1,0:T(8,128)(2,1)S(1)}, u32[]{:S(2)}, u32[]{:S(2)}) collective-permute-start(bf16[32,1024]{1,0:T(8,128)(2,1)S(1)} %maximum_select_fusion.12), channel_id=1, source_target_pairs={{0,16},{8,24},{16,0},{24,8},{32,48},{40,56},{48,32},{56,40},{64,80... | collective-permute-start | bytes 196616 | tf_op jit(solution)/shard_map/while/body/eval_jaxpr/ppermute | solution.py:15
  253.0 7.2 %collective-permute-start.3 = (bf16[32,2048]{1,0:T(8,128)(2,1)S(1)}, bf16[32,2048]{1,0:T(8,128)(2,1)S(1)}, u32[]{:S(2)}, u32[]{:S(2)}) collective-permute-start(bf16[32,2048]{1,0:T(8,128)(2,1)S(1)} %maximum_select_fusion.13), channel_id=1, source_target_pairs={{0,32},{8,40},{16,48},{24,56},{32,0},{40,8},{48,16},{56,24},{64,96... | collective-permute-start | bytes 393224 | tf_op jit(solution)/shard_map/while/body/eval_jaxpr/ppermute | solution.py:15
  260.3 7.1 %collective-permute-start.4 = (bf16[32,4096]{1,0:T(8,128)(2,1)S(1)}, bf16[32,4096]{1,0:T(8,128)(2,1)S(1)}, u32[]{:S(2)}, u32[]{:S(2)}) collective-permute-start(bf16[32,4096]{1,0:T(8,128)(2,1)S(1)} %maximum_select_fusion.14), channel_id=1, source_target_pairs={{0,64},{8,72},{16,80},{24,88},{32,96},{40,104},{48,112},{56,120},{... | collective-permute-start | bytes 786440 | tf_op jit(solution)/shard_map/while/body/eval_jaxpr/ppermute | solution.py:15
  277.2 7.0 %collective-permute-start = (bf16[32,512]{1,0:T(8,128)(2,1)S(1)}, bf16[32,512]{1,0:T(8,128)(2,1)S(1)}, u32[]{:S(2)}, u32[]{:S(2)}) collective-permute-start(bf16[32,512]{1,0:T(8,128)(2,1)S(1)} %broadcast_select_fusion.2), channel_id=1, source_target_pairs={{128,0},{136,8},{144,16},{152,24},{160,32},{168,40},{176,48},{184,... | collective-permute-start | bytes 98312 | tf_op jit(solution)/shard_map/while/body/eval_jaxpr/ppermute | solution.py:21
  284.3 7.4 %collective-permute-start.1 = (bf16[32,512]{1,0:T(8,128)(2,1)S(1)}, bf16[32,512]{1,0:T(8,128)(2,1)S(1)}, u32[]{:S(2)}, u32[]{:S(2)}) collective-permute-start(bf16[32,512]{1,0:T(8,128)(2,1)S(1)} %fusion.30), channel_id=1, source_target_pairs={{0,8},{8,0},{16,24},{24,16},{32,40},{40,32},{48,56},{56,48},{64,72... | collective-permute-start | bytes 98312 | tf_op jit(solution)/shard_map/while/body/eval_jaxpr/ppermute | solution.py:15
  291.8 5.0 %collective-permute-start.2 = (bf16[32,1024]{1,0:T(8,128)(2,1)S(1)}, bf16[32,1024]{1,0:T(8,128)(2,1)S(1)}, u32[]{:S(2)}, u32[]{:S(2)}) collective-permute-start(bf16[32,1024]{1,0:T(8,128)(2,1)S(1)} %maximum_select_fusion.12), channel_id=1, source_target_pairs={{0,16},{8,24},{16,0},{24,8},{32,48},{40,56},{48,32},{56,40},{64,80... | collective-permute-start | bytes 196616 | tf_op jit(solution)/shard_map/while/body/eval_jaxpr/ppermute | solution.py:15
  296.8 7.2 %collective-permute-start.3 = (bf16[32,2048]{1,0:T(8,128)(2,1)S(1)}, bf16[32,2048]{1,0:T(8,128)(2,1)S(1)}, u32[]{:S(2)}, u32[]{:S(2)}) collective-permute-start(bf16[32,2048]{1,0:T(8,128)(2,1)S(1)} %maximum_select_fusion.13), channel_id=1, source_target_pairs={{0,32},{8,40},{16,48},{24,56},{32,0},{40,8},{48,16},{56,24},{64,96... | collective-permute-start | bytes 393224 | tf_op jit(solution)/shard_map/while/body/eval_jaxpr/ppermute | solution.py:15
  304.1 7.1 %collective-permute-start.4 = (bf16[32,4096]{1,0:T(8,128)(2,1)S(1)}, bf16[32,4096]{1,0:T(8,128)(2,1)S(1)}, u32[]{:S(2)}, u32[]{:S(2)}) collective-permute-start(bf16[32,4096]{1,0:T(8,128)(2,1)S(1)} %maximum_select_fusion.14), channel_id=1, source_target_pairs={{0,64},{8,72},{16,80},{24,88},{32,96},{40,104},{48,112},{56,120},{... | collective-permute-start | bytes 786440 | tf_op jit(solution)/shard_map/while/body/eval_jaxpr/ppermute | solution.py:15
  (4 other events, 164.0 us)
Sparse Core Ops, SparseCore 0:
  10.1 102.8 all-gather.1
where the time goes:
time: 348 us; the launch traced here: 347 us
  waiting for transfers between devices  182 us (52%)
  starting transfers between devices  93.4 us (27%)
  matrix products  19 us (5%)
  blocking collectives  18.5 us (5%)
  other arithmetic  15.1 us (4%)
  between operations  14.3 us (4%)
  loops' own time  4.43 us (1%)
    ppermute x24, waiting for transfers between devices, from_partner(): return lax.ppermute(value, axis, pairs)  137 us
    ppermute x24, starting transfers between devices, from_partner(): return lax.ppermute(value, axis, pairs)  86.9 us
    ppermute x5, waiting for transfers between devices, from_behind(): lax.ppermute(value, axis, [(source, source + steps) for source in range(f...  44.5 us
    all_to_all x1, blocking collectives, sent_to_all(): return lax.all_to_all(copies, axis, split_axis=0, concat_axis=0, tiled=True)  18.5 us
    dot_general x2, matrix products, project(): lax.dot_general(gate_full, weight_rows, (((1,), (1,)), ((), ())), preferr...  12 us
    select_n x4, other arithmetic, per_device(): jnp.where(upper_half == 1, jnp.concatenate([partner, right_full], 0), jnp...  7.87 us
  transfers between devices with their start and end apart: 30, of which 29 were waited for; matrix products, arithmetic and copies ran while one was open for 4% of the time, Pallas kernels for 0%

commit v1 on v0

v1 whole, which is shorter than its diff:
```python
import jax
import jax.numpy as jnp
from jax import lax
from jax.experimental import pallas as pl
from jax.experimental.pallas import tpu as pltpu
from jax.sharding import PartitionSpec as P

LAYERS = 4
QUERIES = 16
RANK = 16
CHIPS = 8
MICRO = 4
MESH = pl.DeviceIdType.MESH


def silu_slope(preact):
    sigmoid_value = jax.nn.sigmoid(preact)
    return sigmoid_value * (1.0 + preact * (1.0 - sigmoid_value))


def from_behind(value, axis, steps):
    count = lax.axis_size(axis)
    first, last = (max(0, -steps), min(count, count - steps))
    return lax.ppermute(value, axis, [(source, source + steps) for source in range(first, last)])


def row_scale(lens_ref, rows):
    row = lax.broadcasted_iota(jnp.int32, (rows, 1), 0)
    first, second = lens_ref[0], lens_ref[1]
    count = jnp.where(row < first, first, second).astype(jnp.float32)
    return jnp.where(row < first + second, 1.0 / jnp.maximum(count, 1.0), 0.0)


def backward_kernel(
    lens_ref, cot_ref, pre_ref, w_ref, out_ref,
    cot_v, pre_v, w_v, top_v, pre_t, og, gate_v, gates, part_v, parts, ig, nat,
    load_sem, pre_sem, og_sem, gate_sem, part_sem, nat_sem, send_sem,
):
    position, z = lax.axis_index("section"), lax.axis_index("dp")
    s, c, k = position // 16, (position % 16) // 2, position % 2
    rows, cols = pre_v.shape
    tb = rows // MICRO
    diagonal = c == z

    def device(s_, c_, k_, z_):
        return {"section": s_ * 16 + c_ * 2 + k_, "dp": z_}

    def remote(src, dst, phase, sem, where):
        return pltpu.make_async_remote_copy(
            src_ref=src, dst_ref=dst, send_sem=send_sem.at[phase], recv_sem=sem,
            device_id=where, device_id_type=MESH,
        )

    def arrived(ref, sem):
        pltpu.make_async_copy(ref, ref, sem).wait()

    first_col = pl.multiple_of((c * 2 + k) * cols, cols)
    load_cot = pltpu.make_async_copy(cot_ref.at[:, pl.ds(first_col, cols)], cot_v, load_sem.at[0])
    load_pre = pltpu.make_async_copy(pre_ref, pre_v, load_sem.at[1])
    load_w = pltpu.make_async_copy(w_ref, w_v, load_sem.at[2])
    load_cot.start()
    load_pre.start()
    load_w.start()

    barrier = pltpu.get_barrier_semaphore()

    def greet(where):
        pl.semaphore_signal(barrier, inc=1, device_id=where, device_id_type=MESH)

    def greet_layer(i, carry):
        greet(device(s, (c + i // 2) % CHIPS, (k + i % 2) % 2, z))
        return carry

    lax.fori_loop(1, 2 * CHIPS, greet_layer, 0)

    def greet_column(i, carry):
        @pl.when(jnp.logical_not(diagonal & (i == z)))
        def _():
            greet(device(s, z, k, i))
        return carry

    lax.fori_loop(0, CHIPS, greet_column, 0)

    @pl.when(s < LAYERS - 1)
    def _():
        greet(device(s + 1, c, k, z))

    load_cot.wait()
    load_pre.wait()
    top_v[...] = (cot_v[...].astype(jnp.float32) * row_scale(lens_ref, rows)).astype(jnp.bfloat16)

    expected = 3 * CHIPS - 1 - jnp.where(diagonal, 1, 0) + jnp.where(s > 0, 1, 0)
    pl.semaphore_wait(barrier, expected)

    turned = device(s, z, k, c)

    def turn(src, dst, phase, sem):
        @pl.when(diagonal)
        def _():
            pltpu.make_async_copy(src, dst, sem).start()

        @pl.when(jnp.logical_not(diagonal))
        def _():
            remote(src, dst, phase, sem, turned).start()

    for m in range(MICRO):
        block = pl.ds(m * tb, tb)

        @pl.when(s == LAYERS - 1)
        def _():
            turn(top_v.at[block], og.at[m], 0, og_sem.at[m])

        turn(pre_v.at[block], pre_t.at[m], 1, pre_sem.at[m])

    load_w.wait()

    def spread(m):
        arrived(pre_t.at[m], pre_sem.at[m])
        arrived(og.at[m], og_sem.at[m])
        slope = silu_slope(pre_t[m].astype(jnp.float32))
        gate_v[m] = (slope * og[m].astype(jnp.float32)).astype(jnp.bfloat16)
        slot = gates.at[m, k, c]
        pltpu.make_async_copy(gate_v.at[m], slot, gate_sem.at[m]).start()

        def send(i, carry):
            where = device(s, (c + i // 2) % CHIPS, (k + i % 2) % 2, z)
            remote(gate_v.at[m], slot, 2, gate_sem.at[m], where).start()
            return carry

        lax.fori_loop(1, 2 * CHIPS, send, 0)

    def project(m):
        arrived(gates.at[m], gate_sem.at[m])
        total = None
        for half in range(2):
            gate = gates[m, half].reshape(CHIPS * tb, cols)
            term = lax.dot_general(
                gate, w_v[:, half * cols : (half + 1) * cols],
                (((1,), (1,)), ((), ())), preferred_element_type=jnp.float32,
            )
            total = term if total is None else total + term
        part_v[m] = total.astype(jnp.bfloat16).reshape(CHIPS, tb, w_v.shape[0])

        def send(t, carry):
            here = diagonal & (t == c)
            src, dst = part_v.at[m, t], parts.at[m, z]

            @pl.when(here)
            def _():
                pltpu.make_async_copy(src, dst, part_sem.at[m]).start()

            @pl.when(jnp.logical_not(here))
            def _():
                remote(src, dst, 3, part_sem.at[m], device(s, t, k, c)).start()
            return carry

        lax.fori_loop(0, CHIPS, send, 0)

    def collect(m):
        arrived(parts.at[m], part_sem.at[m])
        total = og[m].astype(jnp.float32)
        back = parts[m, 0].astype(jnp.float32)
        for i in range(1, CHIPS):
            back = back + parts[m, i].astype(jnp.float32)
        ig[m] = (total + back).astype(jnp.bfloat16)

        @pl.when(s > 0)
        def _():
            remote(ig.at[m], og.at[m], 4, og_sem.at[m], device(s - 1, c, k, z)).start()

        turn(ig.at[m], nat.at[m], 5, nat_sem.at[m])

    for step, m in ((0, 0), (0, 1), (1, 0), (0, 2), (1, 1), (0, 3), (1, 2), (1, 3), (2, 0), (2, 1), (2, 2), (2, 3)):
        (spread, project, collect)[step](m)

    for m in range(MICRO):
        arrived(nat.at[m], nat_sem.at[m])
        out_ref[m * tb : (m + 1) * tb] = nat[m]

    @pl.when(jnp.logical_not(diagonal))
    def _():
        @pl.when(s == LAYERS - 1)
        def _():
            arrived(og, send_sem.at[0])

        arrived(pre_t, send_sem.at[1])
        arrived(nat, send_sem.at[5])

    for m in range(MICRO):
        arrived(gates.at[m, 0], send_sem.at[2])
        arrived(gates.at[m, 1, : CHIPS - 1], send_sem.at[2])
        arrived(parts.at[m, : CHIPS - 1], send_sem.at[3])

        @pl.when(jnp.logical_not(diagonal))
        def _():
            arrived(parts.at[m, 0], send_sem.at[3])

    @pl.when(s > 0)
    def _():
        arrived(ig, send_sem.at[4])


def run_backward(lengths, cotangent, preacts, weights):
    rows, cols = preacts.shape
    width = weights.shape[0]
    tb = rows // MICRO
    bf16 = jnp.bfloat16
    anywhere = pl.BlockSpec(memory_space=pl.ANY)
    return pl.pallas_call(
        backward_kernel,
        out_shape=jax.ShapeDtypeStruct((rows, cols), bf16),
        in_specs=[pl.BlockSpec(memory_space=pltpu.SMEM), anywhere, anywhere, anywhere],
        out_specs=pl.BlockSpec(memory_space=pltpu.VMEM),
        scratch_shapes=[
            pltpu.VMEM((rows, cols), bf16),
            pltpu.VMEM((rows, cols), bf16),
            pltpu.VMEM(weights.shape, bf16),
            pltpu.VMEM((rows, cols), bf16),
            pltpu.VMEM((MICRO, tb, cols), bf16),
            pltpu.VMEM((MICRO, tb, cols), bf16),
            pltpu.VMEM((MICRO, tb, cols), bf16),
            pltpu.VMEM((MICRO, 2, CHIPS, tb, cols), bf16),
            pltpu.VMEM((MICRO, CHIPS, tb, width), bf16),
            pltpu.VMEM((MICRO, CHIPS, tb, width), bf16),
            pltpu.VMEM((MICRO, tb, cols), bf16),
            pltpu.VMEM((MICRO, tb, cols), bf16),
            pltpu.SemaphoreType.DMA((3,)),
            pltpu.SemaphoreType.DMA((MICRO,)),
            pltpu.SemaphoreType.DMA((MICRO,)),
            pltpu.SemaphoreType.DMA((MICRO,)),
            pltpu.SemaphoreType.DMA((MICRO,)),
            pltpu.SemaphoreType.DMA((MICRO,)),
            pltpu.SemaphoreType.DMA((6,)),
        ],
        compiler_params=pltpu.CompilerParams(collective_id=0, has_side_effects=True),
    )(lengths, cotangent, preacts, weights)


def per_device(
    cotangent, lengths, example_ids, layer_inputs, preacts, weights, query_left, query_right
):
    per_section = lax.axis_size("section") // LAYERS
    position = lax.axis_index("section")
    section_index, column_block = position // per_section, position % per_section
    group_index = lax.axis_index("dp")
    seq_count, block_cols = lengths.shape[0], layer_inputs.shape[1]
    in_grad = run_backward(lengths, cotangent, preacts, weights)

    seq_slots = group_index * seq_count + jnp.arange(seq_count, dtype=jnp.int32)
    member = (example_ids[:, None] == seq_slots[None, :]).astype(jnp.float32)
    token_len = jnp.dot(member, lengths.astype(jnp.float32), precision=lax.Precision.HIGHEST)
    token_scale = jnp.where(example_ids >= 0, 1.0 / jnp.maximum(token_len, 1.0), 0.0)
    top_columns = lax.dynamic_slice_in_dim(cotangent, column_block * block_cols, block_cols, 1)
    top_grad = (top_columns.astype(jnp.float32) * token_scale[:, None]).astype(jnp.bfloat16)
    arrived = from_behind(in_grad, "section", -per_section)
    out_grad = jnp.where(section_index == LAYERS - 1, top_grad, arrived)
    slope = silu_slope(preacts.astype(jnp.float32))
    gate_grad = (slope * out_grad.astype(jnp.float32)).astype(jnp.bfloat16)
    left = jnp.dot(layer_inputs, query_left, preferred_element_type=jnp.float32)
    right = jnp.dot(gate_grad, query_right, preferred_element_type=jnp.float32)
    groups = [[g * per_section + i for i in range(per_section)] for g in range(LAYERS)]
    both = lax.psum(jnp.concatenate([left, right], axis=1), "section", axis_index_groups=groups)
    product = both[:, : QUERIES * RANK] * both[:, QUERIES * RANK :]
    per_token = jnp.sum(product.reshape(-1, QUERIES, RANK), axis=2)
    scores = jnp.dot(member.T, per_token, precision=lax.Precision.HIGHEST)
    scores = lax.psum(scores, "section") * (1.0 / per_section)
    return (in_grad, scores)


def solution(mesh):
    placed = (
        P("dp", None),
        P("dp"),
        P("dp"),
        P("dp", "section"),
        P("dp", "section"),
        P("section", "dp"),
        P("section", None),
        P("section", None),
    )
    return jax.shard_map(
        per_device,
        mesh=mesh,
        in_specs=placed,
        out_specs=(P("dp", "section"), P("dp", None)),
        check_vma=False,
    )
```

time: 348 us -> 459 us (1.32)
  Pallas kernels: 0 us -> 171 us
  blocking collectives: 18.5 us -> 125 us
  starting transfers between devices: 93.4 us -> 1.46 us
  waiting for transfers between devices: 182 us -> 140 us
  matrix products: 19 us -> 1.67 us
  other arithmetic: 15.1 us -> 2.14 us
    pallas_call x0 -> x1, Pallas kernels: none -> 171 us  [run_backward(): pl.pallas_call(backward_kernel, out_shape=jax.ShapeDtypeStruct((rows, col...]
    ppermute x24 -> x0, waiting for transfers between devices: 137 us -> none  [from_partner(): return lax.ppermute(value, axis, pairs)]
    psum x0 -> x1, waiting for transfers between devices: none -> 136 us  [per_device(): lax.psum(jnp.concatenate([left, right], axis=1), 'section', axis_index_gr...]
    psum x0 -> x1, blocking collectives: none -> 125 us  [per_device(): scores = lax.psum(scores, 'section') * (1.0 / per_section)]
    ppermute x24 -> x0, starting transfers between devices: 86.9 us -> none  [from_partner(): return lax.ppermute(value, axis, pairs)]
    ppermute x5 -> x1, waiting for transfers between devices: 44.5 us -> 3.92 us  [from_behind(): lax.ppermute(value, axis, [(source, source + steps) for source in range(f...]
    all_to_all x1 -> x0, blocking collectives: 18.5 us -> none  [sent_to_all(): return lax.all_to_all(copies, axis, split_axis=0, concat_axis=0, tiled=True)]
    dot_general x8 -> x3, matrix products: 18.8 us -> 1.48 us  [the longest x1 1.07 us: per_device(): right = jnp.dot(gate_grad, query_right, preferred_element_type=jnp.float32)]
  transfers between devices with their start and end apart: 30 -> 2, of which waited for: 29 -> 2; matrix products, arithmetic and copies ran while one was open for 4% -> 0% of each run, Pallas kernels for 0% -> 0%
where the time goes in v1:
time: 459 us; the launch traced here: 456 us
  Pallas kernels  171 us (37%)
  waiting for transfers between devices  140 us (31%)
  blocking collectives  125 us (27%)
  between operations  14.1 us (3%)
    pallas_call x1, Pallas kernels, run_backward(): pl.pallas_call(backward_kernel, out_shape=jax.ShapeDtypeStruct((rows, col...  171 us
    psum x1, waiting for transfers between devices, per_device(): lax.psum(jnp.concatenate([left, right], axis=1), 'section', axis_index_gr...  136 us
    psum x1, blocking collectives, per_device(): scores = lax.psum(scores, 'section') * (1.0 / per_section)  125 us
  transfers between devices with their start and end apart: 2, of which 2 were waited for; matrix products, arithmetic and copies ran while one was open for 0% of the time, Pallas kernels for 0%

profile of v1, /device:TPU:1, one launch (start us, length us, event | category | flops | bytes accessed | tf_op | source)
XLA Modules:
  0.0 456.3 jit_solution(17951839341802148439)
XLA Ops:
  7.2 0.0 copy-start
  7.2 0.0 copy-start.3
  7.2 0.0 all-reduce.2.cloned.1.call-start
  7.2 170.7 %shard_map.95 = bf16[64,512]{1,0:T(8,128)(2,1)} custom-call(s32[2]{0:T(128)} %lens_ref.1, bf16[64,8192]{1,0:T(8,128)(2,1)} %cot_ref.1, bf16[64,512]{1,0:T(8,128)(2,1)} %pre_ref.1, bf16[512,1024]{1,0:T(8,128)(2,1)} %w_ref.1), custom_call_target="tpu_custom_call" | custom-call | tf_op jit(solution)/shard_map/pallas_call | solution.py:209
  178.0 0.0 copy-start.5
  178.0 1.4 collective-permute-start
  179.4 0.0 copy-done
  179.4 0.0 copy-done.3
  179.4 0.0 copy-start.4
  179.5 0.0 copy-start.6
  179.5 0.2 fusion.26
  179.6 0.5 copy-done.4
  180.1 0.0 copy-done.6
  180.1 0.0 copy-start.2
  180.1 0.2 fusion.2
  180.3 3.9 collective-permute-done
  184.2 0.0 copy-done.5
  184.2 0.0 copy-done.2
  184.2 1.1 fusion.10
  185.3 0.7 pad_maximum_fusion
  186.0 0.0 all-reduce.2.cloned.1.call-update
  186.0 136.2 %all-reduce.2.cloned.1.call-done = f32[64,512]{1,0:T(8,128)} async-done(((f32[64,512]{1,0:T(8,128)}), f32[64,512]{1,0:T(8,128)}) %all-reduce.2.cloned.1.call-update) | async-done | bytes 131088 | tf_op jit(solution)/shard_map/psum | solution.py:262
  322.2 0.9 slice_multiply_fusion
  323.0 0.1 copy.11
  323.2 0.0 copy-start.1
  323.2 0.2 fusion.19
  323.4 124.9 %psum.15 = f32[2,16]{1,0:T(2,128)S(1)} all-reduce(f32[2,16]{1,0:T(2,128)S(1)} %fusion.19), channel_id=1, replica_groups=mesh['section'=64,'dp'=8] {'section'}, use_global_device_ids=true, to_apply=%region_2.3 | all-reduce | flops 32 | bytes 256 | tf_op jit(solution)/shard_map/psum | solution.py:266
  448.3 0.6 broadcast_multiply_fusion
  448.9 0.0 copy-done.1
  448.9 0.6 copy.14
  (2 shorter events, 0.0 us)
Async XLA Ops:
  7.2 172.3 %copy-start = (bf16[512,256]{1,0:T(8,128)(2,1)S(1)}, bf16[512,256]{1,0:T(8,128)(2,1)}, u32[]{:S(2)}) copy-start(bf16[512,256]{1,0:T(8,128)(2,1)} %param.14) | copy-start | bytes 786436
  7.2 172.3 %copy-start.3 = (bf16[64,512]{1,0:T(8,128)(2,1)S(1)}, bf16[64,512]{1,0:T(8,128)(2,1)}, u32[]{:S(2)}) copy-start(bf16[64,512]{1,0:T(8,128)(2,1)} %param.11) | copy-start | bytes 196612
  7.2 315.0 %all-reduce.2.cloned.1.call-start = ((), (), s32[]{:S(2)}) async-start(), calls=%async_computation | async-start | bytes 262144 | tf_op jit(solution)/shard_map/psum | solution.py:262
  178.0 6.3 %copy-start.5 = (bf16[512,256]{1,0:T(8,128)(2,1)S(1)}, bf16[512,256]{1,0:T(8,128)(2,1)}, u32[]{:S(2)}) copy-start(bf16[512,256]{1,0:T(8,128)(2,1)} %param.15) | copy-start | bytes 786436
  178.0 6.3 %collective-permute-start = (bf16[64,512]{1,0:T(8,128)(2,1)}, bf16[64,512]{1,0:T(8,128)(2,1)S(1)}, u32[]{:S(2)}, u32[]{:S(2)}) collective-permute-start(bf16[64,512]{1,0:T(8,128)(2,1)} %shard_map.95), channel_id=1, source_target_pairs={{128,0},{136,8},{144,16},{152,24},{160,32},{168,40},{176,48},{184,... | collective-permute-start | bytes 196616 | tf_op jit(solution)/shard_map/ppermute | solution.py:24
  179.4 0.7 copy-start.4
  179.5 0.7 copy-start.6
  180.1 4.1 copy-start.2
  323.2 125.7 %copy-start.1 = (bf16[64,512]{1,0:T(8,128)(2,1)S(1)}, bf16[64,512]{1,0:T(8,128)(2,1)}, u32[]{:S(2)}) copy-start(bf16[64,512]{1,0:T(8,128)(2,1)} %shard_map.95) | copy-start | bytes 196612
Sparse Core Ops, SparseCore 0:
  186.1 136.0 all-reduce.1

commit v2 on v0

v2 whole, which is shorter than its diff:
```python
import jax
import jax.numpy as jnp
from jax import lax
from jax.experimental import pallas as pl
from jax.experimental.pallas import tpu as pltpu
from jax.sharding import PartitionSpec as P

LAYERS = 4
QUERIES = 16
RANK = 16
CHIPS = 8
MICRO = 4
MESH = pl.DeviceIdType.MESH
ORDER = (
    ("s", 0), ("s", 1), ("p", 0), ("s", 2), ("p", 1), ("s", 3), ("p", 2), ("c", 0),
    ("p", 3), ("r", 0), ("c", 1), ("c", 2), ("c", 3), ("r", 1), ("r", 2), ("r", 3),
)


def silu_slope(preact):
    sigmoid_value = jax.nn.sigmoid(preact)
    return sigmoid_value * (1.0 + preact * (1.0 - sigmoid_value))


def influence_kernel(
    lens_ref, cot_ref, in_ref, pre_ref, w_ref, left_ref, right_ref, grads_ref, scores_ref,
    cot_v, in_v, pre_v, w_v, left_v, right_v, low_pre, og, top_gate, next_gate, gates,
    part_v, parts, ig, sides, side_in, per_row, row_in, layer_sum, layer_in,
    load_sem, pre_sem, og_sem, turn_sem, gate_sem, core_sem, part_sem, score_sem, send_sem,
):
    position, z = lax.axis_index("section"), lax.axis_index("dp")
    s, c, k = position // 16, (position % 16) // 2, position % 2
    rows, cols = pre_v.shape
    tb = rows // MICRO
    half = QUERIES * RANK // 2
    top = s == LAYERS - 1
    f32, bf16 = jnp.float32, jnp.bfloat16
    me = c * 2 + k

    def device(s_, c_, k_, z_):
        return {"section": s_ * 16 + c_ * 2 + k_, "dp": z_}

    def in_layer(i):
        return (c + i // 2) % CHIPS, (k + i % 2) % 2

    def remote(src, dst, phase, sem, where):
        pltpu.make_async_remote_copy(
            src_ref=src, dst_ref=dst, send_sem=send_sem.at[phase], recv_sem=sem,
            device_id=where, device_id_type=MESH,
        ).start()

    def arrived(ref, sem):
        pltpu.make_async_copy(ref, ref, sem).wait()

    def each(first, last, body):
        def step(i, carry):
            body(i)
            return carry

        lax.fori_loop(first, last, step, 0)

    first_col = pl.multiple_of(me * cols, cols)
    loads = [
        pltpu.make_async_copy(cot_ref.at[:, pl.ds(first_col, cols)], cot_v, load_sem.at[0]),
        pltpu.make_async_copy(pre_ref, pre_v, load_sem.at[1]),
        pltpu.make_async_copy(w_ref.at[:, pl.ds(0, cols)], w_v.at[0], load_sem.at[2]),
        pltpu.make_async_copy(w_ref.at[:, pl.ds(cols, cols)], w_v.at[1], load_sem.at[3]),
        pltpu.make_async_copy(in_ref, in_v, load_sem.at[4]),
        pltpu.make_async_copy(left_ref, left_v, load_sem.at[5]),
        pltpu.make_async_copy(right_ref, right_v, load_sem.at[6]),
    ]
    for load in loads:
        load.start()

    barrier = pltpu.get_barrier_semaphore()

    def greet(where):
        pl.semaphore_signal(barrier, inc=1, device_id=where, device_id_type=MESH)

    greet(device(jnp.minimum(s + 1, LAYERS - 1), z, k, (c + 6 * z + 7) % CHIPS))
    each(1, LAYERS, lambda i: greet(device((s + i) % LAYERS, c, k, z)))
    each(1, CHIPS, lambda i: greet(device(s, c, k, (z + i) % CHIPS)))
    each(1, 2 * CHIPS, lambda i: greet(device(s, *in_layer(i), z)))

    first, second = lens_ref[0], lens_ref[1]
    row = lax.broadcasted_iota(jnp.int32, (rows, 1), 0)
    count = jnp.where(row < first, first, second).astype(f32)
    scale = jnp.where(row < first + second, 1.0 / jnp.maximum(count, 1.0), 0.0)
    loads[0].wait()
    loads[1].wait()

    @pl.when(top)
    def _():
        for m in range(MICRO):
            block = pl.ds(m * tb, tb)
            top_rows = (cot_v[block].astype(f32) * scale[m * tb : (m + 1) * tb]).astype(bf16)
            og[m] = top_rows
            slope = silu_slope(pre_v[block].astype(f32))
            top_gate[m] = (slope * top_rows.astype(f32)).astype(bf16)

    expected = 2 * CHIPS - 1 + CHIPS - 1 + LAYERS - 1
    expected = expected + jnp.where(s > 0, 1, 0) + jnp.where(top, 1, 0)
    pl.semaphore_wait(barrier, expected)

    turn = (2 * c + z + 1) % CHIPS

    @pl.when(top)
    def _():
        for m in range(MICRO):
            remote(top_gate.at[m], gates.at[m, k, turn], 0, turn_sem.at[m], device(s, turn, k, c))

    @pl.when(s < LAYERS - 1)
    def _():
        remote(pre_v, low_pre, 3, pre_sem.at[0], device(s + 1, c, k, z))

    for load in loads[2:]:
        load.wait()
    left = jnp.dot(in_v[...], left_v[...], preferred_element_type=f32)
    for h in range(2):
        sides[h, :, :half] = left[:, h * half : (h + 1) * half]

    @pl.when(s > 0)
    def _():
        arrived(low_pre, pre_sem.at[0])

    def spread(m):
        mine = gates.at[m, k, c]
        arrived(mine, turn_sem.at[m])
        each(1, CHIPS, lambda i: remote(
            mine, mine, 4, gate_sem.at[m], device(s, (c + i) % CHIPS, k, z)))

    def project(m):
        arrived(gates.at[m, 0, : CHIPS - 1], gate_sem.at[m])
        remote(gates.at[m, k], gates.at[m, k], 5, core_sem.at[m], device(s, c, 1 - k, z))

        def product(h):
            return lax.dot_general(
                gates[m, h].reshape(CHIPS * tb, cols), w_v[h],
                (((1,), (1,)), ((), ())), preferred_element_type=f32,
            )

        total = product(k)
        arrived(gates.at[m, 0], core_sem.at[m])
        total = total + product(1 - k)
        part_v[m] = total.astype(bf16).reshape(CHIPS, tb, cols)

        def send(i):
            t = (z + i) % CHIPS
            remote(part_v.at[m, (t + 2 * z + 1) % CHIPS], parts.at[m, z], 6, part_sem.at[m],
                   device(s, c, k, t))

        each(1, CHIPS, send)
        parts[m, z] = part_v[m, (3 * z + 1) % CHIPS]

        @pl.when(s < LAYERS - 1)
        def _():
            arrived(og.at[m], og_sem.at[m])

    def collect(m):
        arrived(parts.at[m, : CHIPS - 1], part_sem.at[m])
        back = parts[m, 0].astype(f32)
        for i in range(1, CHIPS):
            back = back + parts[m, i].astype(f32)
        in_grad = (og[m].astype(f32) + back).astype(bf16)
        block = pl.ds(m * tb, tb)
        grads_ref[block] = in_grad

        @pl.when(s > 0)
        def _():
            slope = silu_slope(low_pre[block].astype(f32))
            next_gate[m] = (slope * in_grad.astype(f32)).astype(bf16)
            ig[m] = in_grad
            remote(next_gate.at[m], gates.at[m, k, turn], 1, turn_sem.at[m],
                   device(s - 1, turn, k, c))
            remote(ig.at[m], og.at[m], 2, og_sem.at[m], device(s - 1, c, k, z))

    def score(step):
        if step == 0:
            slope = silu_slope(pre_v[...].astype(f32))
            gate = (slope * og[...].reshape(rows, cols).astype(f32)).astype(bf16)
            right = jnp.dot(gate, right_v[...], preferred_element_type=f32)
            for h in range(2):
                sides[h, :, half:] = right[:, h * half : (h + 1) * half]

            def send(i):
                c_, k_ = in_layer(i)
                eight = pl.ds(pl.multiple_of(c_ * 8, 8), 8)
                remote(sides.at[k_, eight], side_in.at[me], 7, score_sem.at[0],
                       device(s, c_, k_, z))

            each(1, 2 * CHIPS, send)
            side_in[me] = sides[k, pl.ds(pl.multiple_of(c * 8, 8), 8)]
        elif step == 1:
            arrived(side_in.at[: 2 * CHIPS - 1], score_sem.at[0])
            both = side_in[0]
            for i in range(1, 2 * CHIPS):
                both = both + side_in[i]
            product = both[:, :half] * both[:, half:]
            eight = lax.broadcasted_iota(jnp.int32, (8, half), 0)
            token = eight + c * 8
            one = jnp.sum(jnp.where(token < first, product, 0.0), axis=0, keepdims=True)
            later = (token >= first) & (token < first + second)
            two = jnp.sum(jnp.where(later, product, 0.0), axis=0, keepdims=True)
            per_row[...] = jnp.where(eight == 0, one, jnp.where(eight == 1, two, 0.0))
            each(1, 2 * CHIPS, lambda i: remote(
                per_row, row_in.at[me], 8, score_sem.at[1], device(s, *in_layer(i), z)))
            row_in[me] = per_row[...]
        elif step == 2:
            arrived(row_in.at[: 2 * CHIPS - 1], score_sem.at[1])
            for h in range(2):
                total = row_in[h]
                for i in range(1, CHIPS):
                    total = total + row_in[2 * i + h]
                layer_sum[:, h * half : (h + 1) * half] = total
            each(1, LAYERS, lambda i: remote(
                layer_sum, layer_in.at[s], 9, score_sem.at[2], device((s + i) % LAYERS, c, k, z)))
            layer_in[s] = layer_sum[...]
        else:
            arrived(layer_in.at[: LAYERS - 1], score_sem.at[2])
            total = layer_in[0]
            for i in range(1, LAYERS):
                total = total + layer_in[i]
            lane = lax.broadcasted_iota(jnp.int32, (2 * half, QUERIES), 0) // RANK
            query = lax.broadcasted_iota(jnp.int32, (2 * half, QUERIES), 1)
            pick = jnp.where(lane == query, 1.0, 0.0).astype(f32)
            summed = jnp.dot(total, pick, precision=lax.Precision.HIGHEST,
                             preferred_element_type=f32)
            scores_ref[...] = summed[: scores_ref.shape[0]]

    events = dict(s=spread, p=project, c=collect, r=score)
    for event, m in ORDER:
        events[event](m)

    @pl.when(top)
    def _():
        arrived(top_gate, send_sem.at[0])

    @pl.when(s > 0)
    def _():
        arrived(next_gate, send_sem.at[1])
        arrived(ig, send_sem.at[2])

    @pl.when(s < LAYERS - 1)
    def _():
        arrived(pre_v, send_sem.at[3])

    arrived(gates.at[:, 0, : CHIPS - 1], send_sem.at[4])
    arrived(gates.at[:, 0], send_sem.at[5])
    arrived(parts.at[:, : CHIPS - 1], send_sem.at[6])
    arrived(side_in.at[: 2 * CHIPS - 1], send_sem.at[7])
    arrived(row_in.at[: 2 * CHIPS - 1], send_sem.at[8])
    arrived(layer_in.at[: LAYERS - 1], send_sem.at[9])


def per_device(
    cotangent, lengths, example_ids, layer_inputs, preacts, weights, query_left, query_right
):
    rows, cols = preacts.shape
    tb = rows // MICRO
    width = QUERIES * RANK
    bf16, f32 = jnp.bfloat16, jnp.float32
    anywhere = pl.BlockSpec(memory_space=pl.ANY)
    in_vmem = pl.BlockSpec(memory_space=pltpu.VMEM)
    chunk = pltpu.VMEM((MICRO, tb, cols), bf16)
    block = pltpu.VMEM((rows, cols), bf16)
    sems = pltpu.SemaphoreType.DMA
    return pl.pallas_call(
        influence_kernel,
        out_shape=(
            jax.ShapeDtypeStruct((rows, cols), bf16),
            jax.ShapeDtypeStruct((lengths.shape[0], QUERIES), f32),
        ),
        in_specs=[pl.BlockSpec(memory_space=pltpu.SMEM)] + [anywhere] * 6,
        out_specs=(in_vmem, in_vmem),
        scratch_shapes=[
            block, block, block,
            pltpu.VMEM((2, cols, cols), bf16),
            pltpu.VMEM(query_left.shape, bf16),
            pltpu.VMEM(query_right.shape, bf16),
            block, chunk, chunk, chunk,
            pltpu.VMEM((MICRO, 2, CHIPS, tb, cols), bf16),
            pltpu.VMEM((MICRO, CHIPS, tb, cols), bf16),
            pltpu.VMEM((MICRO, CHIPS, tb, cols), bf16),
            chunk,
            pltpu.VMEM((2, rows, width), f32),
            pltpu.VMEM((2 * CHIPS, 8, width), f32),
            pltpu.VMEM((8, width // 2), f32),
            pltpu.VMEM((2 * CHIPS, 8, width // 2), f32),
            pltpu.VMEM((8, width), f32),
            pltpu.VMEM((LAYERS, 8, width), f32),
            sems((7,)), sems((1,)), sems((MICRO,)), sems((MICRO,)), sems((MICRO,)),
            sems((MICRO,)), sems((MICRO,)), sems((3,)), sems((10,)),
        ],
        compiler_params=pltpu.CompilerParams(collective_id=0, has_side_effects=True),
    )(lengths, cotangent, layer_inputs, preacts, weights, query_left, query_right)


def solution(mesh):
    placed = (
        P("dp", None),
        P("dp"),
        P("dp"),
        P("dp", "section"),
        P("dp", "section"),
        P("section", "dp"),
        P("section", None),
        P("section", None),
    )
    return jax.shard_map(
        per_device,
        mesh=mesh,
        in_specs=placed,
        out_specs=(P("dp", "section"), P("dp", None)),
        check_vma=False,
    )
```

time: 348 us -> 113 us (0.32)
  waiting for transfers between devices: 182 us -> 0 us
  Pallas kernels: 0 us -> 110 us
  starting transfers between devices: 93.4 us -> 0 us
  matrix products: 19 us -> 0 us
  blocking collectives: 18.5 us -> 0 us
  other arithmetic: 15.1 us -> 0 us
  between operations: 14.3 us -> 0.65 us
  loops' own time: 4.43 us -> 0 us
    ppermute x29 -> x0, waiting for transfers between devices: 181 us -> none  [the longest x24 137 us: from_partner(): return lax.ppermute(value, axis, pairs)]
    pallas_call x0 -> x1, Pallas kernels: none -> 110 us  [per_device(): pl.pallas_call(influence_kernel, out_shape=(jax.ShapeDtypeStruct((rows, c...]
    ppermute x29 -> x0, starting transfers between devices: 93.4 us -> none  [the longest x24 86.9 us: from_partner(): return lax.ppermute(value, axis, pairs)]
    dot_general x9 -> x0, matrix products: 19 us -> none  [the longest x2 12 us: project(): lax.dot_general(gate_full, weight_rows, (((1,), (1,)), ((), ())), preferr...]
    all_to_all x1 -> x0, blocking collectives: 18.5 us -> none  [sent_to_all(): return lax.all_to_all(copies, axis, split_axis=0, concat_axis=0, tiled=True)]
    select_n x29 -> x0, other arithmetic: 9.2 us -> none  [the longest x4 7.87 us: per_device(): jnp.where(upper_half == 1, jnp.concatenate([partner, right_full], 0), jnp...]
    another operation x11 -> x0, loops' own time: 4.43 us -> none  [the longest x1 4.16 us: per_device(): lax.fori_loop(0, step_count, advance, initial)]
    reduce_or x5 -> x0, other arithmetic: 3.95 us -> none  [advance(): has_live = in_range & jnp.any(id_rows >= 0)]
  transfers between devices with their start and end apart: 30 -> 0, of which waited for: 29 -> 0; matrix products, arithmetic and copies ran while one was open for 4% -> 0% of each run, Pallas kernels for 0% -> 0%
where the time goes in v2:
time: 113 us; the launch traced here: 112 us
  Pallas kernels  110 us (97%)
  local copies, waits for them, and re-layouts  2.04 us (2%)
    pallas_call x1, Pallas kernels, per_device(): pl.pallas_call(influence_kernel, out_shape=(jax.ShapeDtypeStruct((rows, c...  110 us

profile of v2, /device:TPU:1, one launch (start us, length us, event | category | flops | bytes accessed | tf_op | source)
XLA Modules:
  0.0 112.3 jit_solution(11163656537113417986)
XLA Ops:
  0.6 109.6 %shard_map.86 = (bf16[64,512]{1,0:T(8,128)(2,1)}, f32[2,16]{1,0:T(2,128)}) custom-call(s32[2]{0:T(128)} %lens_ref.1, bf16[64,8192]{1,0:T(8,128)(2,1)} %cot_ref.1, bf16[64,512]{1,0:T(8,128)(2,1)} %in_ref.1, bf16[64,512]{1,0:T(8,128)(2,1)} %pre_ref.1, bf16[512,1024]{1,0:T(8,128)(2,1)} %w_ref.1, bf16[512,256]{1,0:T(8,128)(2,1)} %left_ref.1, ...), custom_call_target="tpu_custom_call" | custom-call | tf_op jit(solution)/shard_map/pallas_call | solution.py:267
  110.2 0.0 copy-start
  110.3 1.5 %copy.11 = bf16[64,512]{1,0:T(8,128)(2,1)} copy(bf16[64,512]{1,0:T(8,128)(2,1)} %get-tuple-element.4) | data formatting | bytes 131072
  111.7 0.0 copy-done
  111.7 0.6 copy.12
Async XLA Ops:
  110.2 1.5 %copy-start = (f32[2,16]{1,0:T(2,128)S(1)}, f32[2,16]{1,0:T(2,128)}, u32[]{:S(2)}) copy-start(f32[2,16]{1,0:T(2,128)} %get-tuple-element.5) | copy-start | bytes 388

commit v3 on v2

--- a/solution.py
+++ b/solution.py
@@ -12,9 +12,10 @@
 MICRO = 4
 MESH = pl.DeviceIdType.MESH
 ORDER = (
-    ("s", 0), ("s", 1), ("p", 0), ("s", 2), ("p", 1), ("s", 3), ("p", 2), ("c", 0),
-    ("p", 3), ("r", 0), ("c", 1), ("c", 2), ("c", 3), ("r", 1), ("r", 2), ("r", 3),
+    ("s", 0), ("s", 1), ("p", 0), ("s", 2), ("p", 1), ("e", 0), ("s", 3), ("p", 2), ("e", 1), ("c", 0),
+    ("p", 3), ("c", 1), ("e", 2), ("c", 2), ("c", 3), ("l", 0), ("l", 1), ("l", 2), ("r", 3),
 )
+ROUTE = ((0, 2), (0, 1), (0, 0), (1, 1), (1, 0), (1, 3), (1, 2), (0, 3))
 
 
 def silu_slope(preact):
@@ -22,9 +23,29 @@
     return sigmoid_value * (1.0 + preact * (1.0 - sigmoid_value))
 
 
+def looked_up(table, index):
+    value = jnp.int32(table[0])
+    for i in range(1, len(table)):
+        value = jnp.where(index == i, table[i], value)
+    return value
+
+
+def chip_of(plane, source):
+    away = (source + CHIPS - plane) % CHIPS
+    row, step = (looked_up([pair[i] for pair in ROUTE], away) for i in range(2))
+    return row * 4 + (plane + step) % 4
+
+
+def source_of(plane, chip):
+    away = [0] * CHIPS
+    for i, (row, step) in enumerate(ROUTE):
+        away[row * 4 + step] = i
+    return (plane + looked_up(away, chip // 4 * 4 + (chip + 4 - plane % 4) % 4)) % CHIPS
+
+
 def influence_kernel(
     lens_ref, cot_ref, in_ref, pre_ref, w_ref, left_ref, right_ref, grads_ref, scores_ref,
-    cot_v, in_v, pre_v, w_v, left_v, right_v, low_pre, og, top_gate, next_gate, gates,
+    cot_v, in_v, pre_v, w_v, left_v, right_v, low_pre, low_slope, own_slope, og, top_gate, next_gate, gates,
     part_v, parts, ig, sides, side_in, per_row, row_in, layer_sum, layer_in,
     load_sem, pre_sem, og_sem, turn_sem, gate_sem, core_sem, part_sem, score_sem, send_sem,
 ):
@@ -77,7 +98,7 @@
     def greet(where):
         pl.semaphore_signal(barrier, inc=1, device_id=where, device_id_type=MESH)
 
-    greet(device(jnp.minimum(s + 1, LAYERS - 1), z, k, (c + 6 * z + 7) % CHIPS))
+    greet(device(jnp.minimum(s + 1, LAYERS - 1), z, k, source_of(z, c)))
     each(1, LAYERS, lambda i: greet(device((s + i) % LAYERS, c, k, z)))
     each(1, CHIPS, lambda i: greet(device(s, c, k, (z + i) % CHIPS)))
     each(1, 2 * CHIPS, lambda i: greet(device(s, *in_layer(i), z)))
@@ -102,7 +123,7 @@
     expected = expected + jnp.where(s > 0, 1, 0) + jnp.where(top, 1, 0)
     pl.semaphore_wait(barrier, expected)
 
-    turn = (2 * c + z + 1) % CHIPS
+    turn = chip_of(c, z)
 
     @pl.when(top)
     def _():
@@ -118,10 +139,12 @@
     left = jnp.dot(in_v[...], left_v[...], preferred_element_type=f32)
     for h in range(2):
         sides[h, :, :half] = left[:, h * half : (h + 1) * half]
+    own_slope[...] = silu_slope(pre_v[...].astype(f32))
 
     @pl.when(s > 0)
     def _():
         arrived(low_pre, pre_sem.at[0])
+        low_slope[...] = silu_slope(low_pre[...].astype(f32))
 
     def spread(m):
         mine = gates.at[m, k, c]
@@ -146,17 +169,19 @@
 
         def send(i):
             t = (z + i) % CHIPS
-            remote(part_v.at[m, (t + 2 * z + 1) % CHIPS], parts.at[m, z], 6, part_sem.at[m],
+            remote(part_v.at[m, chip_of(z, t)], parts.at[m, z], 6, part_sem.at[m],
                    device(s, c, k, t))
 
         each(1, CHIPS, send)
-        parts[m, z] = part_v[m, (3 * z + 1) % CHIPS]
-
-        @pl.when(s < LAYERS - 1)
+        parts[m, z] = part_v[m, chip_of(z, z)]
+
+    def wait_residual(m, which):
+        @pl.when(which)
         def _():
             arrived(og.at[m], og_sem.at[m])
 
     def collect(m):
+        wait_residual(m, (s > 0) & (s < LAYERS - 1))
         arrived(parts.at[m, : CHIPS - 1], part_sem.at[m])
         back = parts[m, 0].astype(f32)
         for i in range(1, CHIPS):
@@ -167,8 +192,7 @@
 
         @pl.when(s > 0)
         def _():
-            slope = silu_slope(low_pre[block].astype(f32))
-            next_gate[m] = (slope * in_grad.astype(f32)).astype(bf16)
+            next_gate[m] = (low_slope[block] * in_grad.astype(f32)).astype(bf16)
             ig[m] = in_grad
             remote(next_gate.at[m], gates.at[m, k, turn], 1, turn_sem.at[m],
                    device(s - 1, turn, k, c))
@@ -176,8 +200,9 @@
 
     def score(step):
         if step == 0:
-            slope = silu_slope(pre_v[...].astype(f32))
-            gate = (slope * og[...].reshape(rows, cols).astype(f32)).astype(bf16)
+            for m in range(MICRO):
+                wait_residual(m, s == 0)
+            gate = (own_slope[...] * og[...].reshape(rows, cols).astype(f32)).astype(bf16)
             right = jnp.dot(gate, right_v[...], preferred_element_type=f32)
             for h in range(2):
                 sides[h, :, half:] = right[:, h * half : (h + 1) * half]
@@ -227,7 +252,17 @@
                              preferred_element_type=f32)
             scores_ref[...] = summed[: scores_ref.shape[0]]
 
-    events = dict(s=spread, p=project, c=collect, r=score)
+    def early(step):
+        @pl.when(s == 0)
+        def _():
+            score(step)
+
+    def late(step):
+        @pl.when(s > 0)
+        def _():
+            score(step)
+
+    events = dict(s=spread, p=project, c=collect, r=score, e=early, l=late)
     for event, m in ORDER:
         events[event](m)
 
@@ -277,7 +312,7 @@
             pltpu.VMEM((2, cols, cols), bf16),
             pltpu.VMEM(query_left.shape, bf16),
             pltpu.VMEM(query_right.shape, bf16),
-            block, chunk, chunk, chunk,
+            block, pltpu.VMEM((rows, cols), f32), pltpu.VMEM((rows, cols), f32), chunk, chunk, chunk,
             pltpu.VMEM((MICRO, 2, CHIPS, tb, cols), bf16),
             pltpu.VMEM((MICRO, CHIPS, tb, cols), bf16),
             pltpu.VMEM((MICRO, CHIPS, tb, cols), bf16),

time: 113 us -> 102 us (0.903)
  Pallas kernels: 110 us -> 99.2 us
    pallas_call x1, Pallas kernels: 110 us -> 99.2 us  [per_device(): pl.pallas_call(influence_kernel, out_shape=(jax.ShapeDtypeStruct((rows, c...]
where the time goes in v3:
time: 102 us
  Pallas kernels  99.2 us (97%)
  local copies, waits for them, and re-layouts  2.04 us (2%)
    pallas_call x1, Pallas kernels, per_device(): pl.pallas_call(influence_kernel, out_shape=(jax.ShapeDtypeStruct((rows, c...  99.2 us

profile of v3, /device:TPU:1, one launch (start us, length us, event | category | flops | bytes accessed | tf_op | source)
XLA Modules:
  0.0 101.9 jit_solution(9629248155832346853)
XLA Ops:
  0.6 99.2 %shard_map.86 = (bf16[64,512]{1,0:T(8,128)(2,1)}, f32[2,16]{1,0:T(2,128)}) custom-call(s32[2]{0:T(128)} %lens_ref.1, bf16[64,8192]{1,0:T(8,128)(2,1)} %cot_ref.1, bf16[64,512]{1,0:T(8,128)(2,1)} %in_ref.1, bf16[64,512]{1,0:T(8,128)(2,1)} %pre_ref.1, bf16[512,1024]{1,0:T(8,128)(2,1)} %w_ref.1, bf16[512,256]{1,0:T(8,128)(2,1)} %left_ref.1, ...), custom_call_target="tpu_custom_call" | custom-call | tf_op jit(solution)/shard_map/pallas_call | solution.py:302
  99.8 0.0 copy-start
  99.8 1.5 %copy.11 = bf16[64,512]{1,0:T(8,128)(2,1)} copy(bf16[64,512]{1,0:T(8,128)(2,1)} %get-tuple-element.4) | data formatting | bytes 131072
  101.3 0.0 copy-done
  101.3 0.6 copy.12
Async XLA Ops:
  99.8 1.5 %copy-start = (f32[2,16]{1,0:T(2,128)S(1)}, f32[2,16]{1,0:T(2,128)}, u32[]{:S(2)}) copy-start(f32[2,16]{1,0:T(2,128)} %get-tuple-element.5) | copy-start | bytes 388

commit v4 on v3

--- a/solution.py
+++ b/solution.py
@@ -9,11 +9,10 @@
 QUERIES = 16
 RANK = 16
 CHIPS = 8
-MICRO = 4
+MICRO = 8
 MESH = pl.DeviceIdType.MESH
 ORDER = (
-    ("s", 0), ("s", 1), ("p", 0), ("s", 2), ("p", 1), ("e", 0), ("s", 3), ("p", 2), ("e", 1), ("c", 0),
-    ("p", 3), ("c", 1), ("e", 2), ("c", 2), ("c", 3), ("l", 0), ("l", 1), ("l", 2), ("r", 3),
+    ("s", 0), ("s", 1), ("s", 2), ("s", 3), ("x", 0), ("s", 4), ("x", 1), ("p", 0), ("s", 5), ("x", 2), ("p", 1), ("s", 6), ("x", 3), ("p", 2), ("e", 0), ("s", 7), ("x", 4), ("p", 3), ("x", 5), ("c", 0), ("p", 4), ("x", 6), ("c", 1), ("p", 5), ("x", 7), ("c", 2), ("p", 6), ("e", 1), ("c", 3), ("p", 7), ("c", 4), ("c", 5), ("e", 2), ("c", 6), ("c", 7), ("l", 0), ("l", 1), ("l", 2), ("r", 3),
 )
 ROUTE = ((0, 2), (0, 1), (0, 0), (1, 1), (1, 0), (1, 3), (1, 2), (0, 3))
 
@@ -46,7 +45,7 @@
 def influence_kernel(
     lens_ref, cot_ref, in_ref, pre_ref, w_ref, left_ref, right_ref, grads_ref, scores_ref,
     cot_v, in_v, pre_v, w_v, left_v, right_v, low_pre, low_slope, own_slope, og, top_gate, next_gate, gates,
-    part_v, parts, ig, sides, side_in, per_row, row_in, layer_sum, layer_in,
+    half_product, part_v, parts, ig, sides, side_in, per_row, row_in, layer_sum, layer_in,
     load_sem, pre_sem, og_sem, turn_sem, gate_sem, core_sem, part_sem, score_sem, send_sem,
 ):
     position, z = lax.axis_index("section"), lax.axis_index("dp")
@@ -124,6 +123,13 @@
     pl.semaphore_wait(barrier, expected)
 
     turn = chip_of(c, z)
+    plane_peers = [
+        s * 16 + ((c // 4 + row) % 2 * 4 + (c + step) % 4) * 2 + k
+        for row, step in ((1, 2), (0, 2), (1, 1), (1, 3), (0, 1), (0, 3), (1, 0))
+    ]
+    slots = [row * 4 + (z + step) % 4 for row, step in ROUTE]
+    own_slot = slots[0]
+    column_peers = [((z + i) % CHIPS, slots[i]) for i in (4, 3, 5, 2, 6, 1, 7)]
 
     @pl.when(top)
     def _():
@@ -139,6 +145,8 @@
     left = jnp.dot(in_v[...], left_v[...], preferred_element_type=f32)
     for h in range(2):
         sides[h, :, :half] = left[:, h * half : (h + 1) * half]
+    for h in range(2):
+        w_v[h] = w_v[h].T
     own_slope[...] = silu_slope(pre_v[...].astype(f32))
 
     @pl.when(s > 0)
@@ -149,31 +157,28 @@
     def spread(m):
         mine = gates.at[m, k, c]
         arrived(mine, turn_sem.at[m])
-        each(1, CHIPS, lambda i: remote(
-            mine, mine, 4, gate_sem.at[m], device(s, (c + i) % CHIPS, k, z)))
-
-    def project(m):
+        for peer in plane_peers:
+            remote(mine, mine, 4, gate_sem.at[m], {"section": peer, "dp": z})
+
+    def product(m, h):
+        gate = gates[m, h].reshape(CHIPS * tb, cols)
+        return jnp.dot(gate, w_v[h], preferred_element_type=f32)
+
+    def exchange(m):
         arrived(gates.at[m, 0, : CHIPS - 1], gate_sem.at[m])
         remote(gates.at[m, k], gates.at[m, k], 5, core_sem.at[m], device(s, c, 1 - k, z))
 
-        def product(h):
-            return lax.dot_general(
-                gates[m, h].reshape(CHIPS * tb, cols), w_v[h],
-                (((1,), (1,)), ((), ())), preferred_element_type=f32,
-            )
-
-        total = product(k)
+        half_product[m] = product(m, k)
+
+    def project(m):
         arrived(gates.at[m, 0], core_sem.at[m])
-        total = total + product(1 - k)
+        total = half_product[m] + product(m, 1 - k)
         part_v[m] = total.astype(bf16).reshape(CHIPS, tb, cols)
 
-        def send(i):
-            t = (z + i) % CHIPS
-            remote(part_v.at[m, chip_of(z, t)], parts.at[m, z], 6, part_sem.at[m],
-                   device(s, c, k, t))
-
-        each(1, CHIPS, send)
-        parts[m, z] = part_v[m, chip_of(z, z)]
+        for t, slot in column_peers:
+            remote(part_v.at[m, slot], parts.at[m, z], 6, part_sem.at[m],
+                   {"section": position, "dp": t})
+        parts[m, z] = part_v[m, own_slot]
 
     def wait_residual(m, which):
         @pl.when(which)
@@ -262,7 +267,7 @@
         def _():
             score(step)
 
-    events = dict(s=spread, p=project, c=collect, r=score, e=early, l=late)
+    events = dict(s=spread, x=exchange, p=project, c=collect, r=score, e=early, l=late)
     for event, m in ORDER:
         events[event](m)
 
@@ -314,6 +319,7 @@
             pltpu.VMEM(query_right.shape, bf16),
             block, pltpu.VMEM((rows, cols), f32), pltpu.VMEM((rows, cols), f32), chunk, chunk, chunk,
             pltpu.VMEM((MICRO, 2, CHIPS, tb, cols), bf16),
+            pltpu.VMEM((MICRO, CHIPS * tb, cols), f32),
             pltpu.VMEM((MICRO, CHIPS, tb, cols), bf16),
             pltpu.VMEM((MICRO, CHIPS, tb, cols), bf16),
             chunk,

time: 102 us -> 95.1 us (0.932)
  Pallas kernels: 99.2 us -> 92.2 us
    pallas_call x1, Pallas kernels: 99.2 us -> 92.2 us  [per_device(): pl.pallas_call(influence_kernel, out_shape=(jax.ShapeDtypeStruct((rows, c...]
where the time goes in v4:
time: 95.1 us; the launch traced here: 94.9 us
  Pallas kernels  92.2 us (97%)
  local copies, waits for them, and re-layouts  2.04 us (2%)
    pallas_call x1, Pallas kernels, per_device(): pl.pallas_call(influence_kernel, out_shape=(jax.ShapeDtypeStruct((rows, c...  92.2 us
    unnamed x4, local copies, waits for them, and re-layouts  2.04 us

profile of v4, /device:TPU:1, one launch (start us, length us, event | category | flops | bytes accessed | tf_op | source)
XLA Modules:
  0.0 94.9 jit_solution(11108606507657765593)
XLA Ops:
  0.6 92.2 %shard_map.86 = (bf16[64,512]{1,0:T(8,128)(2,1)}, f32[2,16]{1,0:T(2,128)}) custom-call(s32[2]{0:T(128)} %lens_ref.1, bf16[64,8192]{1,0:T(8,128)(2,1)} %cot_ref.1, bf16[64,512]{1,0:T(8,128)(2,1)} %in_ref.1, bf16[64,512]{1,0:T(8,128)(2,1)} %pre_ref.1, bf16[512,1024]{1,0:T(8,128)(2,1)} %w_ref.1, bf16[512,256]{1,0:T(8,128)(2,1)} %left_ref.1, ...), custom_call_target="tpu_custom_call" | custom-call | tf_op jit(solution)/shard_map/pallas_call | solution.py:307
  92.8 0.0 copy-start
  92.8 1.5 %copy.11 = bf16[64,512]{1,0:T(8,128)(2,1)} copy(bf16[64,512]{1,0:T(8,128)(2,1)} %get-tuple-element.4) | data formatting | bytes 131072
  94.3 0.0 copy-done
  94.3 0.6 copy.12
Async XLA Ops:
  92.8 1.5 %copy-start = (f32[2,16]{1,0:T(2,128)S(1)}, f32[2,16]{1,0:T(2,128)}, u32[]{:S(2)}) copy-start(f32[2,16]{1,0:T(2,128)} %get-tuple-element.5) | copy-start | bytes 388

commit v5 on v4

--- a/solution.py
+++ b/solution.py
@@ -12,9 +12,9 @@
 MICRO = 8
 MESH = pl.DeviceIdType.MESH
 ORDER = (
-    ("s", 0), ("s", 1), ("s", 2), ("s", 3), ("x", 0), ("s", 4), ("x", 1), ("p", 0), ("s", 5), ("x", 2), ("p", 1), ("s", 6), ("x", 3), ("p", 2), ("e", 0), ("s", 7), ("x", 4), ("p", 3), ("x", 5), ("c", 0), ("p", 4), ("x", 6), ("c", 1), ("p", 5), ("x", 7), ("c", 2), ("p", 6), ("e", 1), ("c", 3), ("p", 7), ("c", 4), ("c", 5), ("e", 2), ("c", 6), ("c", 7), ("l", 0), ("l", 1), ("l", 2), ("r", 3),
+    ("s", 0), ("s", 1), ("s", 2), ("s", 3), ("x", 0), ("p", 0), ("s", 4), ("x", 1), ("p", 1), ("s", 5), ("x", 2), ("p", 2), ("s", 6), ("x", 3), ("p", 3), ("s", 7), ("x", 4), ("e", 0), ("c", 0), ("p", 4), ("x", 5), ("c", 1), ("p", 5), ("x", 6), ("c", 2), ("p", 6), ("e", 1), ("x", 7), ("c", 3), ("p", 7), ("c", 4), ("c", 5), ("e", 2), ("c", 6), ("c", 7), ("l", 0), ("l", 1), ("l", 2), ("r", 3),
 )
-ROUTE = ((0, 2), (0, 1), (0, 0), (1, 1), (1, 0), (1, 3), (1, 2), (0, 3))
+ROUTE = ((0, 2), (0, 3), (0, 0), (1, 3), (1, 0), (1, 1), (1, 2), (0, 1))
 
 
 def silu_slope(preact):

time: 95.1 us -> 93.9 us (0.987)
  Pallas kernels: 92.2 us -> 91 us
    pallas_call x1, Pallas kernels: 92.2 us -> 91 us  [per_device(): pl.pallas_call(influence_kernel, out_shape=(jax.ShapeDtypeStruct((rows, c...]
where the time goes in v5:
time: 93.9 us; the launch traced here: 93.7 us
  Pallas kernels  91 us (97%)
  local copies, waits for them, and re-layouts  2.04 us (2%)
    pallas_call x1, Pallas kernels, per_device(): pl.pallas_call(influence_kernel, out_shape=(jax.ShapeDtypeStruct((rows, c...  91 us
    unnamed x4, local copies, waits for them, and re-layouts  2.04 us

profile of v5, /device:TPU:1, one launch (start us, length us, event | category | flops | bytes accessed | tf_op | source)
XLA Modules:
  0.0 93.7 jit_solution(17805739503635115307)
XLA Ops:
  0.6 91.0 %shard_map.86 = (bf16[64,512]{1,0:T(8,128)(2,1)}, f32[2,16]{1,0:T(2,128)}) custom-call(s32[2]{0:T(128)} %lens_ref.1, bf16[64,8192]{1,0:T(8,128)(2,1)} %cot_ref.1, bf16[64,512]{1,0:T(8,128)(2,1)} %in_ref.1, bf16[64,512]{1,0:T(8,128)(2,1)} %pre_ref.1, bf16[512,1024]{1,0:T(8,128)(2,1)} %w_ref.1, bf16[512,256]{1,0:T(8,128)(2,1)} %left_ref.1, ...), custom_call_target="tpu_custom_call" | custom-call | tf_op jit(solution)/shard_map/pallas_call | solution.py:307
  91.7 0.0 copy-start
  91.7 1.5 %copy.11 = bf16[64,512]{1,0:T(8,128)(2,1)} copy(bf16[64,512]{1,0:T(8,128)(2,1)} %get-tuple-element.4) | data formatting | bytes 131072
  93.1 0.0 copy-done
  93.2 0.6 copy.12
Async XLA Ops:
  91.7 1.5 %copy-start = (f32[2,16]{1,0:T(2,128)S(1)}, f32[2,16]{1,0:T(2,128)}, u32[]{:S(2)}) copy-start(f32[2,16]{1,0:T(2,128)} %get-tuple-element.5) | copy-start | bytes 388
